TPU v7x, 512 devices: a whole 4x8x8 slice. The times are simulated.
512 devices in a mesh: rows: 32 (over z_lo, y), cols: 16 (over x, z_hi, core).
Axes of the slice: x: 4, y: 8, z: 8 (z_hi: 2, z_lo: 4; z = z_hi * 4 + z_lo), core: 2. Of those that a mesh axis runs over, the one named last changes fastest.
Arguments:
- series: float32 [2097152], P(('rows', 'cols')), may hold values from -6 to 6
- tile_list: int32 [3, 2048], P(None, 'rows'), may hold values from 0 to 4094, as said below
Outputs:
- profile: float32 [2097152], P(('rows', 'cols'))
Inputs may be any that keep to these rules, and one draw needn't show every extreme that they name: The columns of tile_list lying on one index of rows list 64 distinct tiles (row block, offset) of that row group: the row block lies in the group, the offset is below 8, and row block plus offset is at most 4094. Every group but the last lists a tile whose column block lies in the next group; the last group lists the tile of row block 4094 and offset 0. The third row is an index of cols; in each group no index owns more than 8 tiles and one owns exactly 8.
All inputs are finite; a program needn't handle non-finite values.
Results may differ from a plain program's by a relative error of at most 0.0001.
Values sent between devices are 32-bit elements; how exact they have to be, the bound alone decides.
A program may use at most 64 MiB of HBM per device.

v0:
```python
import math

import jax
import jax.numpy as jnp
from jax import lax
from jax.sharding import PartitionSpec as P

M = 256
B = 512
BPR = 128
CAP = 8
NEXT = 4096
EXCL = 64


def passed_along(block, axis, distance):
    devices = range(lax.axis_size(axis))
    route = [(i - distance, i) for i in devices if i - distance in devices]
    return lax.ppermute(block, axis, route)


def hankel(values, rows, width):
    length = values.shape[0]
    flat = jnp.concatenate([jnp.tile(values, rows), jnp.zeros((rows,), values.dtype)])
    return flat.reshape(rows, length + 1)[:, :width]


def normalize(values):
    windows = hankel(values, B, M)
    centre = windows - jnp.mean(windows, axis=1, keepdims=True)
    spread = jnp.mean(centre * centre, axis=1)
    factor = lax.rsqrt(spread + 1e-05) / math.sqrt(M)
    return centre * factor[:, None]


def tile_maxima(left_data, right_data, offset):
    left_z = normalize(left_data)
    right_z = normalize(right_data)
    corr = lax.dot_general(
        left_z,
        right_z,
        (((1,), (1,)), ((), ())),
        precision=lax.Precision.HIGHEST,
        preferred_element_type=jnp.float32,
    )
    row_pos = lax.broadcasted_iota(jnp.int32, (B, B), 0)
    col_pos = lax.broadcasted_iota(jnp.int32, (B, B), 1)
    keep = offset * B + col_pos - row_pos >= EXCL
    corr = jnp.where(keep, corr, jnp.float32(-1.0))
    return (jnp.max(corr, axis=1), jnp.max(corr, axis=0))


def raise_block(partial_max, start, values):
    current = lax.dynamic_slice_in_dim(partial_max, start, B)
    return lax.dynamic_update_slice_in_dim(partial_max, jnp.maximum(current, values), start, 0)


def on_device(series, tile_list):
    piece = series.shape[0]
    col_count = lax.axis_size("cols")
    seg_len = piece * col_count
    group = lax.axis_index("rows")
    col_id = lax.axis_index("cols")
    segment = lax.all_gather(series, "cols", axis=0, tiled=True)
    head = passed_along(segment[:NEXT], "rows", -1)
    signal = jnp.concatenate([segment, head])
    foreign = (tile_list[2] != col_id).astype(jnp.int32)
    order = jnp.argsort(foreign, stable=True)[:CAP]
    live = tile_list[2][order] == col_id
    slots = CAP
    partial_max = jnp.full((seg_len + NEXT,), -1.0, jnp.float32)

    def step(index, partial_max):
        which = order[index]
        local_block = tile_list[0, which] - group * BPR
        offset = tile_list[1, which]
        row_start = local_block * B
        col_start = (local_block + offset) * B
        left_data = lax.dynamic_slice_in_dim(signal, row_start, B + M)
        right_data = lax.dynamic_slice_in_dim(signal, col_start, B + M)
        row_max, col_max = tile_maxima(left_data, right_data, offset)
        active = live[index]
        row_max = jnp.where(active, row_max, jnp.float32(-1.0))
        col_max = jnp.where(active, col_max, jnp.float32(-1.0))
        partial_max = raise_block(partial_max, row_start, row_max)
        return raise_block(partial_max, col_start, col_max)

    partial_max = lax.fori_loop(0, slots, step, partial_max)
    own_part = partial_max[:seg_len]
    spill = partial_max[seg_len:]
    own_part, spill = lax.pmax((own_part, spill), "cols")
    arrived = passed_along(spill, "rows", 1)
    arrived = jnp.where(group > 0, arrived, jnp.float32(-1.0))
    own_part = jnp.concatenate([jnp.maximum(own_part[:NEXT], arrived), own_part[NEXT:]])
    return lax.dynamic_slice_in_dim(own_part, col_id * piece, piece)


def solution(mesh):
    in_specs = (P(("rows", "cols")), P(None, "rows"))
    out_specs = P(("rows", "cols"))
    return jax.shard_map(
        on_device, mesh=mesh, in_specs=in_specs, out_specs=out_specs, check_vma=False
    )
```

profile of v0, /device:TPU:1, one launch (start us, length us, event | category | flops | bytes accessed | tf_op | source)
XLA Modules:
  0.0 393.7 jit_solution(1997206631718759267)
XLA Ops:
  6.5 37.6 %all_gather.3 = f32[65536]{0:T(1024)S(1)} all-gather(f32[4096]{0:T(1024)} %param.4), channel_id=1, replica_groups=mesh['rows'=32,'cols'=16] {'cols'}, dimensions={0}, use_global_device_ids=true | all-gather | bytes 278528 | tf_op jit(solution)/shard_map/all_gather | solution.py:64
  46.8 2.0 sort.17
  50.3 152.8 %while.15 = (s32[]{:T(128)}, f32[69632]{0:T(1024)}, s32[8]{0:T(128)S(1)}, s32[3,64]{1,0:T(4,128)}, s32[]{:T(128)}, /*index=5*/pred[8]{0:T(512)(128)(4,1)S(1)}, f...) while((s32[]{:T(128)}, f32[69632]{0:T(1024)}, ...), condition=%wide.region_8.9_spmd, body=%wide.region_1.8_spmd.sunk | while | flops 808193536 | bytes 33783220 | solution.py:88
  61.9 2.4 fusion.12
  65.0 2.2 maximum_dynamic-update-slice_fusion.4
  67.2 2.2 maximum_dynamic-update-slice_fusion.5
  81.0 2.4 fusion.12
  84.1 2.2 maximum_dynamic-update-slice_fusion.4
  86.3 2.2 maximum_dynamic-update-slice_fusion.5
  100.1 2.4 fusion.12
  103.2 2.2 maximum_dynamic-update-slice_fusion.4
  105.4 2.2 maximum_dynamic-update-slice_fusion.5
  119.2 2.4 fusion.12
  122.2 2.2 maximum_dynamic-update-slice_fusion.4
  124.4 2.2 maximum_dynamic-update-slice_fusion.5
  135.7 1.6 reshape.63
  138.3 2.4 fusion.12
  141.3 2.2 maximum_dynamic-update-slice_fusion.4
  143.5 2.2 maximum_dynamic-update-slice_fusion.5
  157.4 2.4 fusion.12
  160.4 2.2 maximum_dynamic-update-slice_fusion.4
  162.6 2.2 maximum_dynamic-update-slice_fusion.5
  176.5 2.4 fusion.12
  179.5 2.2 maximum_dynamic-update-slice_fusion.4
  181.7 2.2 maximum_dynamic-update-slice_fusion.5
  195.6 2.4 fusion.12
  198.6 2.2 maximum_dynamic-update-slice_fusion.4
  200.8 2.2 maximum_dynamic-update-slice_fusion.5
  203.0 1.7 slice.43
  205.5 76.3 %pmax.15 = f32[4096]{0:T(1024)S(1)} all-reduce(f32[4096]{0:T(1024)S(1)} %slice.45), channel_id=1, replica_groups=mesh['rows'=32,'cols'=16] {'cols'}, use_global_device_ids=true, to_apply=%region_10.11 | all-reduce | flops 4096 | bytes 32768 | tf_op jit(solution)/shard_map/pmax | solution.py:91
  281.8 4.0 %collective-permute-start.1 = (f32[4096]{0:T(1024)S(1)}, f32[4096]{0:T(1024)S(1)}, u32[]{:S(2)}, u32[]{:S(2)}) collective-permute-start(f32[4096]{0:T(1024)S(1)} %pmax.15), channel_id=1, source_target_pairs={{0,16},{16,32},{32,48},{48,64},{64,80},{80,96},{96,112},{112,128},... | collective-permute-start | bytes 49160 | tf_op jit(solution)/shard_map/ppermute | solution.py:19
  285.8 98.8 %all-reduce.4.cloned.1.call-done = f32[65536]{0:T(1024)} async-done(((f32[65536]{0:T(1024)}), f32[65536]{0:T(1024)}) %all-reduce.4.cloned.1.call-update) | async-done | bytes 262160 | tf_op jit(solution)/shard_map/pmax | solution.py:91
  (226 shorter events, 71.7 us)
Async XLA Ops:
  6.5 378.0 %all-reduce.4.cloned.1.call-start = ((), (), s32[]{:S(2)}) async-start(), calls=%async_computation | async-start | bytes 524288 | tf_op jit(solution)/shard_map/pmax | solution.py:91
  44.1 5.4 %collective-permute-start = (f32[4096]{0:T(1024)S(1)}, f32[4096]{0:T(1024)S(1)}, u32[]{:S(2)}, u32[]{:S(2)}) collective-permute-start(f32[4096]{0:T(1024)S(1)} %slice.51), channel_id=1, source_target_pairs={{16,0},{32,16},{48,32},{64,48},{80,64},{96,80},{112,96},{128,112},... | collective-permute-start | bytes 49160 | tf_op jit(solution)/shard_map/ppermute | solution.py:19
  50.3 5.5 %copy-start.1 = (f32[69632]{0:T(1024)}, f32[69632]{0:T(1024)S(1)}, u32[]{:S(2)}) copy-start(f32[69632]{0:T(1024)S(1)} %get-tuple-element.293) | copy-start | bytes 835588 | tf_op jit(solution)/shard_map/while
  57.7 1.3 copy-start
  60.9 8.5 %copy-start.2 = (f32[69632]{0:T(1024)S(1)}, f32[69632]{0:T(1024)}, u32[]{:S(2)}) copy-start(f32[69632]{0:T(1024)} %copy-done.1) | copy-start | bytes 835588 | tf_op jit(solution)/shard_map/while
  69.4 5.5 %copy-start.1 = (f32[69632]{0:T(1024)}, f32[69632]{0:T(1024)S(1)}, u32[]{:S(2)}) copy-start(f32[69632]{0:T(1024)S(1)} %get-tuple-element.293) | copy-start | bytes 835588 | tf_op jit(solution)/shard_map/while
  76.8 1.3 copy-start
  80.0 8.5 %copy-start.2 = (f32[69632]{0:T(1024)S(1)}, f32[69632]{0:T(1024)}, u32[]{:S(2)}) copy-start(f32[69632]{0:T(1024)} %copy-done.1) | copy-start | bytes 835588 | tf_op jit(solution)/shard_map/while
  88.5 5.5 %copy-start.1 = (f32[69632]{0:T(1024)}, f32[69632]{0:T(1024)S(1)}, u32[]{:S(2)}) copy-start(f32[69632]{0:T(1024)S(1)} %get-tuple-element.293) | copy-start | bytes 835588 | tf_op jit(solution)/shard_map/while
  95.9 1.3 copy-start
  99.1 8.5 %copy-start.2 = (f32[69632]{0:T(1024)S(1)}, f32[69632]{0:T(1024)}, u32[]{:S(2)}) copy-start(f32[69632]{0:T(1024)} %copy-done.1) | copy-start | bytes 835588 | tf_op jit(solution)/shard_map/while
  107.6 5.5 %copy-start.1 = (f32[69632]{0:T(1024)}, f32[69632]{0:T(1024)S(1)}, u32[]{:S(2)}) copy-start(f32[69632]{0:T(1024)S(1)} %get-tuple-element.293) | copy-start | bytes 835588 | tf_op jit(solution)/shard_map/while
  115.0 1.3 copy-start
  118.2 8.5 %copy-start.2 = (f32[69632]{0:T(1024)S(1)}, f32[69632]{0:T(1024)}, u32[]{:S(2)}) copy-start(f32[69632]{0:T(1024)} %copy-done.1) | copy-start | bytes 835588 | tf_op jit(solution)/shard_map/while
  126.7 5.5 %copy-start.1 = (f32[69632]{0:T(1024)}, f32[69632]{0:T(1024)S(1)}, u32[]{:S(2)}) copy-start(f32[69632]{0:T(1024)S(1)} %get-tuple-element.293) | copy-start | bytes 835588 | tf_op jit(solution)/shard_map/while
  134.1 1.3 copy-start
  137.3 8.5 %copy-start.2 = (f32[69632]{0:T(1024)S(1)}, f32[69632]{0:T(1024)}, u32[]{:S(2)}) copy-start(f32[69632]{0:T(1024)} %copy-done.1) | copy-start | bytes 835588 | tf_op jit(solution)/shard_map/while
  145.8 5.5 %copy-start.1 = (f32[69632]{0:T(1024)}, f32[69632]{0:T(1024)S(1)}, u32[]{:S(2)}) copy-start(f32[69632]{0:T(1024)S(1)} %get-tuple-element.293) | copy-start | bytes 835588 | tf_op jit(solution)/shard_map/while
  153.2 1.3 copy-start
  156.4 8.5 %copy-start.2 = (f32[69632]{0:T(1024)S(1)}, f32[69632]{0:T(1024)}, u32[]{:S(2)}) copy-start(f32[69632]{0:T(1024)} %copy-done.1) | copy-start | bytes 835588 | tf_op jit(solution)/shard_map/while
  164.8 5.5 %copy-start.1 = (f32[69632]{0:T(1024)}, f32[69632]{0:T(1024)S(1)}, u32[]{:S(2)}) copy-start(f32[69632]{0:T(1024)S(1)} %get-tuple-element.293) | copy-start | bytes 835588 | tf_op jit(solution)/shard_map/while
  172.3 1.3 copy-start
  175.5 8.5 %copy-start.2 = (f32[69632]{0:T(1024)S(1)}, f32[69632]{0:T(1024)}, u32[]{:S(2)}) copy-start(f32[69632]{0:T(1024)} %copy-done.1) | copy-start | bytes 835588 | tf_op jit(solution)/shard_map/while
  183.9 5.5 %copy-start.1 = (f32[69632]{0:T(1024)}, f32[69632]{0:T(1024)S(1)}, u32[]{:S(2)}) copy-start(f32[69632]{0:T(1024)S(1)} %get-tuple-element.293) | copy-start | bytes 835588 | tf_op jit(solution)/shard_map/while
  191.4 1.3 copy-start
  194.6 8.5 %copy-start.2 = (f32[69632]{0:T(1024)S(1)}, f32[69632]{0:T(1024)}, u32[]{:S(2)}) copy-start(f32[69632]{0:T(1024)} %copy-done.1) | copy-start | bytes 835588 | tf_op jit(solution)/shard_map/while
  281.8 103.8 %collective-permute-start.1 = (f32[4096]{0:T(1024)S(1)}, f32[4096]{0:T(1024)S(1)}, u32[]{:S(2)}, u32[]{:S(2)}) collective-permute-start(f32[4096]{0:T(1024)S(1)} %pmax.15), channel_id=1, source_target_pairs={{0,16},{16,32},{32,48},{48,64},{64,80},{80,96},{96,112},{112,128},... | collective-permute-start | bytes 49160 | tf_op jit(solution)/shard_map/ppermute | solution.py:19
Sparse Core Ops, SparseCore 0:
  204.9 179.6 all-reduce.3
where the time goes:
time: 397 us; the launch traced here: 394 us
  blocking collectives  114 us (29%)
  waiting for transfers between devices  98.8 us (25%)
  local copies, waits for them, and re-layouts  65.3 us (16%)
  other arithmetic  45.5 us (11%)
  loops' own time  32.2 us (8%)
  matrix products  19.3 us (5%)
  between operations  13.5 us (3%)
  starting transfers between devices  5.3 us (1%)
    pmax x1, waiting for transfers between devices, on_device(): own_part, spill = lax.pmax((own_part, spill), 'cols')  98.8 us
    pmax x1, blocking collectives, on_device(): own_part, spill = lax.pmax((own_part, spill), 'cols')  76.3 us
    all_gather x1, blocking collectives, on_device(): segment = lax.all_gather(series, 'cols', axis=0, tiled=True)  37.6 us
    dynamic_update_slice x16, other arithmetic, raise_block(): lax.dynamic_update_slice_in_dim(partial_max, jnp.maximum(current, values)...  35.2 us
    another operation x1, loops' own time, on_device(): partial_max = lax.fori_loop(0, slots, step, partial_max)  32.2 us
    reshape x16, local copies, waits for them, and re-layouts, hankel(): return flat.reshape(rows, length + 1)[:, :width]  25.1 us
    dot_general x8, matrix products, tile_maxima(): lax.dot_general(left_z, right_z, (((1,), (1,)), ((), ())), precision=lax....  19.3 us
    dynamic_slice x8, local copies, waits for them, and re-layouts, step(): offset = tile_list[1, which]  11.4 us
  transfers between devices with their start and end apart: 3, of which 1 were waited for; matrix products, arithmetic and copies ran while one was open for 1% of the time, Pallas kernels for 0%

commit v1 on v0

v1 whole, which is shorter than its diff:
```python
import math

import jax
import jax.numpy as jnp
from jax import lax
from jax.experimental import pallas as pl
from jax.experimental.pallas import tpu as pltpu
from jax.sharding import PartitionSpec as P

M = 256
B = 512
BPR = 128
EXCL = 64
SPILL = 8
SEG = B + M


def passed_along(block, axis, distance):
    devices = range(lax.axis_size(axis))
    route = [(i - distance, i) for i in devices if i - distance in devices]
    return lax.ppermute(block, axis, route)


def windows(row):
    wide = jnp.broadcast_to(row, (B, SEG))
    rolled = pltpu.roll(wide, 0, 1, stride=1, stride_axis=0)
    w = rolled[:, B:SEG]
    centre = w - jnp.mean(w, axis=1, keepdims=True)
    spread = jnp.mean(centre * centre, axis=1, keepdims=True)
    factor = lax.rsqrt(spread + 1e-05) / math.sqrt(M)
    return centre * factor


def tile_kernel(n_tiles, idx_ref, blocks_ref, out_ref):
    out_ref[...] = jnp.full(out_ref.shape, -1.0, jnp.float32)
    q = lax.broadcasted_iota(jnp.int32, (B, B), 0)
    s = lax.broadcasted_iota(jnp.int32, (B, B), 1)

    def body(t, carry):
        i = idx_ref[0, t]
        d = idx_ref[1, t]
        j = i + d
        zl = windows(blocks_ref[pl.ds(i, 1), :])
        zr = windows(blocks_ref[pl.ds(j, 1), :])
        corr = lax.dot_general(
            zl,
            zr,
            (((1,), (1,)), ((), ())),
            precision=lax.Precision.HIGHEST,
            preferred_element_type=jnp.float32,
        )
        corr = jnp.where(d * B + s - q >= EXCL, corr, jnp.float32(-1.0))
        col_max = jnp.max(corr, axis=0, keepdims=True)
        row_max_c = jnp.max(corr, axis=1, keepdims=True)
        row_max = jnp.sum(jnp.where(q == s, row_max_c, 0.0), axis=0, keepdims=True)
        out_ref[pl.ds(i, 1), :] = jnp.maximum(out_ref[pl.ds(i, 1), :], row_max)
        out_ref[pl.ds(j, 1), :] = jnp.maximum(out_ref[pl.ds(j, 1), :], col_max)
        return carry

    lax.fori_loop(0, n_tiles, body, 0)


def tile_maxima(idx, blocks):
    n_tiles = idx.shape[1]
    n_blocks = blocks.shape[0]
    return pl.pallas_call(
        lambda *refs: tile_kernel(n_tiles, *refs),
        out_shape=jax.ShapeDtypeStruct((n_blocks, B), jnp.float32),
        in_specs=[
            pl.BlockSpec(memory_space=pltpu.SMEM),
            pl.BlockSpec(memory_space=pltpu.VMEM),
        ],
        out_specs=pl.BlockSpec(memory_space=pltpu.VMEM),
        cost_estimate=pl.CostEstimate(
            flops=n_tiles * 2 * B * B * M * 6,
            bytes_accessed=n_blocks * (SEG + B) * 4,
            transcendentals=n_tiles * 2 * B,
        ),
    )(idx, blocks)


def on_device(series, tile_list):
    piece = series.shape[0]
    col_count = lax.axis_size("cols")
    group = lax.axis_index("rows")
    col_id = lax.axis_index("cols")
    segment = lax.all_gather(series, "cols", axis=0, tiled=True)
    head = passed_along(segment[: SPILL * B], "rows", -1)
    signal = jnp.concatenate([segment, head, jnp.zeros((B,), jnp.float32)])
    n_blocks = BPR + SPILL
    by_block = signal.reshape(n_blocks + 1, B)
    blocks = jnp.concatenate([by_block[:n_blocks], by_block[1:, :M]], axis=1)[:, ::-1]

    per_dev = tile_list.shape[1] // col_count
    mine = lax.dynamic_slice_in_dim(
        tile_list[:2].reshape(2, per_dev, col_count), col_id, 1, axis=2
    )[:, :, 0]
    idx = jnp.stack([mine[0] - group * BPR, mine[1]])

    partial = tile_maxima(idx, blocks)
    own = partial[:BPR]
    spill = partial[BPR:]
    arrived = passed_along(spill, "rows", 1)
    arrived = jnp.where(group > 0, arrived, jnp.float32(-1.0))
    own = jnp.concatenate([jnp.maximum(own[:SPILL], arrived), own[SPILL:]])
    chunks = own.reshape(col_count, BPR // col_count, B)
    got = lax.all_to_all(chunks, "cols", 0, 0, tiled=True)
    result = jnp.max(got.reshape(col_count, BPR // col_count, B), axis=0)
    return result.reshape(piece)


def solution(mesh):
    in_specs = (P(("rows", "cols")), P(None, "rows"))
    out_specs = P(("rows", "cols"))
    return jax.shard_map(
        on_device, mesh=mesh, in_specs=in_specs, out_specs=out_specs, check_vma=False
    )
```

time: 397 us -> 83.7 us (0.21)
  the two profiles are of different devices: /device:TPU:1 before, /device:TPU:88 now
where the time goes in v1:
time: 83.7 us; the launch traced here: 83.5 us
  blocking collectives  52.9 us (63%)
  Pallas kernels  12 us (14%)
  local copies, waits for them, and re-layouts  6.63 us (8%)
  starting transfers between devices  5.81 us (7%)
  waiting for transfers between devices  5.04 us (6%)
  other arithmetic  0.91 us (1%)
    all_gather x1, blocking collectives, on_device(): segment = lax.all_gather(series, 'cols', axis=0, tiled=True)  35.6 us
    all_to_all x1, blocking collectives, on_device(): got = lax.all_to_all(chunks, 'cols', 0, 0, tiled=True)  17.4 us
    pallas_call x1, Pallas kernels, tile_maxima(): pl.pallas_call(lambda *refs: tile_kernel(n_tiles, *refs), out_shape=jax.S...  12 us
    ppermute x2, starting transfers between devices, passed_along(): return lax.ppermute(block, axis, route)  5.81 us
    ppermute x2, waiting for transfers between devices, passed_along(): return lax.ppermute(block, axis, route)  5.04 us
    rev x1, local copies, waits for them, and re-layouts, on_device(): jnp.concatenate([by_block[:n_blocks], by_block[1:, :M]], axis=1)[:, ::-1]  4.36 us
  transfers between devices with their start and end apart: 2, of which 2 were waited for; matrix products, arithmetic and copies ran while one was open for 1% of the time, Pallas kernels for 0%

profile of v1, /device:TPU:88, one launch (start us, length us, event | category | flops | bytes accessed | tf_op | source)
XLA Modules:
  0.0 83.5 jit_solution(5606488421782119452)
XLA Ops:
  0.0 35.6 %all_gather.3 = f32[65536]{0:T(1024)S(1)} all-gather(f32[4096]{0:T(1024)} %param.2), channel_id=1, replica_groups=mesh['rows'=32,'cols'=16] {'cols'}, dimensions={0}, use_global_device_ids=true | all-gather | bytes 278528 | tf_op jit(solution)/shard_map/all_gather | solution.py:87
  35.6 2.3 %collective-permute-start = (f32[4096]{0:T(1024)S(1)}, f32[4096]{0:T(1024)S(1)}, u32[]{:S(2)}, u32[]{:S(2)}) collective-permute-start(f32[4096]{0:T(1024)S(1)} %slice.48), channel_id=1, source_target_pairs={{16,0},{32,16},{48,32},{64,48},{80,64},{96,80},{112,96},{128,112},... | collective-permute-start | bytes 49160 | tf_op jit(solution)/shard_map/ppermute | solution.py:21
  37.9 0.0 slice-start.1
  37.9 0.7 slice-done.1
  38.6 0.1 reshape.30
  38.7 0.2 fusion
  38.9 0.6 pad_add_fusion.refs_0_
  39.5 2.9 %collective-permute-done = f32[4096]{0:T(1024)S(1)} collective-permute-done((f32[4096]{0:T(1024)S(1)}, f32[4096]{0:T(1024)S(1)}, u32[]{:S(2)}, u32[]{:S(2)}) %collective-permute-start) | collective-permute-done | bytes 16416 | tf_op jit(solution)/shard_map/ppermute | solution.py:21
  42.6 4.4 %rev.3.refs_1_ = f32[136,768]{1,0:T(8,128)} reverse(f32[136,768]{1,0:T(8,128)S(1)} %pad_maximum_fusion), dimensions={1} | reverse | bytes 835584 | tf_op jit(solution)/shard_map/rev | solution.py:92
  47.0 12.0 %shard_map.28 = f32[136,512]{1,0:T(8,128)} custom-call(s32[2,4]{1,0:T(2,128)} %pad_add_fusion.refs_0_, f32[136,768]{1,0:T(8,128)} %rev.3.refs_1_), custom_call_target="tpu_custom_call" | custom-call | flops 3221225472 | bytes 696320 | tf_op jit(solution)/shard_map/pallas_call | solution.py:66
  59.0 0.0 copy-start
  59.0 0.8 slice.51
  59.8 3.5 %collective-permute-start.1 = (f32[8,512]{1,0:T(8,128)S(1)}, f32[8,512]{1,0:T(8,128)S(1)}, u32[]{:S(2)}, u32[]{:S(2)}) collective-permute-start(f32[8,512]{1,0:T(8,128)S(1)} %slice.51), channel_id=1, source_target_pairs={{0,16},{16,32},{32,48},{48,64},{64,80},{80,96},{96,112},{112,128},... | collective-permute-start | bytes 49160 | tf_op jit(solution)/shard_map/ppermute | solution.py:21
  63.3 0.0 slice-start
  63.3 2.1 %collective-permute-done.1 = f32[8,512]{1,0:T(8,128)S(1)} collective-permute-done((f32[8,512]{1,0:T(8,128)S(1)}, f32[8,512]{1,0:T(8,128)S(1)}, u32[]{:S(2)}, u32[]{:S(2)}) %collective-permute-start.1) | collective-permute-done | bytes 16416 | tf_op jit(solution)/shard_map/ppermute | solution.py:21
  65.4 0.0 copy-done
  65.4 0.0 slice-done
  65.5 17.4 %all_to_all.5 = f32[16,8,512]{2,1,0:T(8,128)S(1)} all-to-all(f32[16,8,512]{2,1,0:T(8,128)S(1)} %maximum_bitcast_fusion), channel_id=1, replica_groups=mesh['rows'=32,'cols'=16] {'cols'}, dimensions={0} | all-to-all | bytes 524288 | tf_op jit(solution)/shard_map/all_to_all | solution.py:107
  82.8 0.6 copy.3
  (11 shorter events, 0.2 us)
Async XLA Ops:
  35.6 6.8 %collective-permute-start = (f32[4096]{0:T(1024)S(1)}, f32[4096]{0:T(1024)S(1)}, u32[]{:S(2)}, u32[]{:S(2)}) collective-permute-start(f32[4096]{0:T(1024)S(1)} %slice.48), channel_id=1, source_target_pairs={{16,0},{32,16},{48,32},{64,48},{80,64},{96,80},{112,96},{128,112},... | collective-permute-start | bytes 49160 | tf_op jit(solution)/shard_map/ppermute | solution.py:21
  37.9 0.7 slice-start.1
  59.0 6.4 %copy-start = (f32[136,512]{1,0:T(8,128)S(1)}, f32[136,512]{1,0:T(8,128)}, u32[]{:S(2)}) copy-start(f32[136,512]{1,0:T(8,128)} %shard_map.28) | copy-start | bytes 835588
  59.8 5.6 %collective-permute-start.1 = (f32[8,512]{1,0:T(8,128)S(1)}, f32[8,512]{1,0:T(8,128)S(1)}, u32[]{:S(2)}, u32[]{:S(2)}) collective-permute-start(f32[8,512]{1,0:T(8,128)S(1)} %slice.51), channel_id=1, source_target_pairs={{0,16},{16,32},{32,48},{48,64},{64,80},{80,96},{96,112},{112,128},... | collective-permute-start | bytes 49160 | tf_op jit(solution)/shard_map/ppermute | solution.py:21
  63.3 2.2 %slice-start = ((f32[136,512]{1,0:T(8,128)}), f32[120,512]{1,0:T(8,128)S(1)}, s32[]{:S(2)}) async-start(f32[136,512]{1,0:T(8,128)} %shard_map.28), calls=%async_computation.1 | async-start | bytes 491520 | tf_op jit(solution)/shard_map/slice | solution.py:105

commit v2 on v1

--- a/solution.py
+++ b/solution.py
@@ -13,6 +13,7 @@
 EXCL = 64
 SPILL = 8
 SEG = B + M
+MESH = pl.DeviceIdType.MESH
 
 
 def passed_along(block, axis, distance):
@@ -79,14 +80,122 @@
     )(idx, blocks)
 
 
+def greet_partners(n_rows, n_cols):
+    g = lax.axis_index("rows")
+    c = lax.axis_index("cols")
+    barrier = pltpu.get_barrier_semaphore()
+    for p in range(n_cols):
+        @pl.when(p != c)
+        def _():
+            pl.semaphore_signal(barrier, 1, device_id=(g, p), device_id_type=MESH)
+
+    @pl.when(g + 1 < n_rows)
+    def _():
+        pl.semaphore_signal(barrier, 1, device_id=(g + 1, 0), device_id_type=MESH)
+
+    first = jnp.logical_and(c == 0, g > 0)
+
+    @pl.when(first)
+    def _():
+        for p in range(n_cols):
+            pl.semaphore_signal(barrier, 1, device_id=(g - 1, p), device_id_type=MESH)
+
+    count = (n_cols - 1) + (g + 1 < n_rows).astype(jnp.int32) + n_cols * first.astype(jnp.int32)
+    pl.semaphore_wait(barrier, count)
+    return g, c, first
+
+
+def gather_kernel(n_rows, n_cols, piece_ref, out_ref, held, send_sems, recv_sems):
+    g, c, first = greet_partners(n_rows, n_cols)
+
+    def to_peer(p):
+        return pltpu.make_async_remote_copy(
+            src_ref=piece_ref,
+            dst_ref=held.at[c],
+            send_sem=send_sems.at[p],
+            recv_sem=recv_sems.at[c],
+            device_id=(g, p),
+            device_id_type=MESH,
+        )
+
+    def from_peer(p):
+        return pltpu.make_async_remote_copy(
+            src_ref=piece_ref,
+            dst_ref=held.at[p],
+            send_sem=send_sems.at[p],
+            recv_sem=recv_sems.at[p],
+            device_id=(g, p),
+            device_id_type=MESH,
+        )
+
+    def head_to(p):
+        return pltpu.make_async_remote_copy(
+            src_ref=piece_ref,
+            dst_ref=held.at[n_cols],
+            send_sem=send_sems.at[n_cols + p],
+            recv_sem=recv_sems.at[n_cols],
+            device_id=(g - 1, p),
+            device_id_type=MESH,
+        )
+
+    @pl.when(first)
+    def _():
+        for p in range(n_cols):
+            head_to(p).start()
+
+    for p in range(n_cols):
+        @pl.when(p != c)
+        def _():
+            to_peer(p).start()
+
+    held[pl.ds(c, 1)] = piece_ref[...][None]
+
+    @pl.when(g + 1 == n_rows)
+    def _():
+        held[n_cols] = jnp.zeros(piece_ref.shape, jnp.float32)
+
+    for p in range(n_cols):
+        @pl.when(p != c)
+        def _():
+            from_peer(p).wait_recv()
+            to_peer(p).wait_send()
+
+    @pl.when(g + 1 < n_rows)
+    def _():
+        head_to(0).wait_recv()
+
+    @pl.when(first)
+    def _():
+        for p in range(n_cols):
+            head_to(p).wait_send()
+
+    out_ref[...] = held[...]
+
+
+def gather_group(piece, n_rows, n_cols):
+    shape = (n_cols + 1,) + piece.shape
+    return pl.pallas_call(
+        lambda *refs: gather_kernel(n_rows, n_cols, *refs),
+        out_shape=jax.ShapeDtypeStruct(shape, jnp.float32),
+        in_specs=[pl.BlockSpec(memory_space=pltpu.VMEM)],
+        out_specs=pl.BlockSpec(memory_space=pltpu.VMEM),
+        scratch_shapes=[
+            pltpu.VMEM(shape, jnp.float32),
+            pltpu.SemaphoreType.DMA((2 * n_cols,)),
+            pltpu.SemaphoreType.DMA((n_cols + 1,)),
+        ],
+        compiler_params=pltpu.CompilerParams(collective_id=0, has_side_effects=True),
+    )(piece)
+
+
 def on_device(series, tile_list):
     piece = series.shape[0]
     col_count = lax.axis_size("cols")
     group = lax.axis_index("rows")
     col_id = lax.axis_index("cols")
-    segment = lax.all_gather(series, "cols", axis=0, tiled=True)
-    head = passed_along(segment[: SPILL * B], "rows", -1)
-    signal = jnp.concatenate([segment, head, jnp.zeros((B,), jnp.float32)])
+    n_rows = lax.axis_size("rows")
+    held = gather_group(series.reshape(SPILL, B), n_rows, col_count)
+    signal = jnp.concatenate([held.reshape(-1), jnp.zeros((B,), jnp.float32)])
     n_blocks = BPR + SPILL
     by_block = signal.reshape(n_blocks + 1, B)
     blocks = jnp.concatenate([by_block[:n_blocks], by_block[1:, :M]], axis=1)[:, ::-1]

time: 83.7 us -> 77.2 us (0.922)
  the two profiles are of different devices: /device:TPU:88 before, /device:TPU:64 now
where the time goes in v2:
time: 77.2 us; the launch traced here: 76.7 us
  Pallas kernels  34.6 us (45%)
  blocking collectives  24.3 us (31%)
  local copies, waits for them, and re-layouts  9.21 us (12%)
  waiting for transfers between devices  4.65 us (6%)
  starting transfers between devices  3.05 us (4%)
  other arithmetic  0.87 us (1%)
    all_to_all x1, blocking collectives, on_device(): got = lax.all_to_all(chunks, 'cols', 0, 0, tiled=True)  24.3 us
    pallas_call x1, Pallas kernels, gather_group(): pl.pallas_call(lambda *refs: gather_kernel(n_rows, n_cols, *refs), out_sh...  22.6 us
    pallas_call x1, Pallas kernels, tile_maxima(): pl.pallas_call(lambda *refs: tile_kernel(n_tiles, *refs), out_shape=jax.S...  12 us
    ppermute x1, waiting for transfers between devices, passed_along(): return lax.ppermute(block, axis, route)  4.65 us
    rev x1, local copies, waits for them, and re-layouts, on_device(): jnp.concatenate([by_block[:n_blocks], by_block[1:, :M]], axis=1)[:, ::-1]  4.37 us
    ppermute x1, starting transfers between devices, passed_along(): return lax.ppermute(block, axis, route)  3.05 us
    unnamed x8, local copies, waits for them, and re-layouts  2.57 us
  transfers between devices with their start and end apart: 1, of which 1 were waited for; matrix products, arithmetic and copies ran while one was open for 0% of the time, Pallas kernels for 0%

profile of v2, /device:TPU:64, one launch (start us, length us, event | category | flops | bytes accessed | tf_op | source)
XLA Modules:
  0.0 76.7 jit_solution(9215219565134105901)
XLA Ops:
  0.0 0.0 copy-start.2
  0.0 0.0 slice-start.1
  0.0 0.7 slice-done.1
  0.7 0.1 reshape.37
  0.8 0.0 copy-done.2
  0.8 0.6 reshape.38.refs_0_
  1.4 22.6 %shard_map.28 = f32[17,8,512]{2,1,0:T(8,128)} custom-call(f32[8,512]{1,0:T(8,128)} %reshape.38.refs_0_), custom_call_target="tpu_custom_call" | custom-call | tf_op jit(solution)/shard_map/pallas_call | solution.py:177
  24.0 1.0 %copy.3 = f32[17,4,8,128]{3,1,2,0:T(4,128)S(1)} copy(f32[17,4,8,128]{3,2,1,0:T(8,128)} %bitcast.9) | data formatting | bytes 557056
  25.1 0.0 copy-start
  25.1 0.9 %copy-done = f32[17,8,512]{2,1,0:T(8,128)S(1)} copy-done((f32[17,8,512]{2,1,0:T(8,128)S(1)}, f32[17,8,512]{2,1,0:T(8,128)}, u32[]{:S(2)}) %copy-start) | copy-done | bytes 278552
  26.1 4.4 %rev.3.refs_1_ = f32[136,768]{1,0:T(8,128)} reverse(f32[136,768]{1,0:T(8,128)S(1)} %pad_maximum_fusion), dimensions={1} | reverse | bytes 835584 | tf_op jit(solution)/shard_map/rev | solution.py:201
  30.4 0.2 fusion
  30.6 0.6 pad_add_fusion.refs_0_
  31.2 12.0 %shard_map.29 = f32[136,512]{1,0:T(8,128)} custom-call(s32[2,4]{1,0:T(2,128)} %pad_add_fusion.refs_0_, f32[136,768]{1,0:T(8,128)} %rev.3.refs_1_), custom_call_target="tpu_custom_call" | custom-call | flops 3221225472 | bytes 696320 | tf_op jit(solution)/shard_map/pallas_call | solution.py:67
  43.2 0.0 copy-start.1
  43.2 0.8 %slice.45 = f32[8,512]{1,0:T(8,128)S(1)} slice(f32[136,512]{1,0:T(8,128)} %shard_map.29), slice={[128:136], [0:512]} | slice | bytes 32768 | tf_op jit(solution)/shard_map/slice | solution.py:211
  44.0 3.1 %collective-permute-start = (f32[8,512]{1,0:T(8,128)S(1)}, f32[8,512]{1,0:T(8,128)S(1)}, u32[]{:S(2)}, u32[]{:S(2)}) collective-permute-start(f32[8,512]{1,0:T(8,128)S(1)} %slice.45), channel_id=1, source_target_pairs={{0,16},{16,32},{32,48},{48,64},{64,80},{80,96},{96,112},{112,128},... | collective-permute-start | bytes 49160 | tf_op jit(solution)/shard_map/ppermute | solution.py:22
  47.1 0.0 slice-start
  47.1 4.7 %collective-permute-done = f32[8,512]{1,0:T(8,128)S(1)} collective-permute-done((f32[8,512]{1,0:T(8,128)S(1)}, f32[8,512]{1,0:T(8,128)S(1)}, u32[]{:S(2)}, u32[]{:S(2)}) %collective-permute-start) | collective-permute-done | bytes 16416 | tf_op jit(solution)/shard_map/ppermute | solution.py:22
  51.7 0.0 copy-done.1
  51.8 0.0 slice-done
  51.8 24.3 %all_to_all.5 = f32[16,8,512]{2,1,0:T(8,128)S(1)} all-to-all(f32[16,8,512]{2,1,0:T(8,128)S(1)} %maximum_bitcast_fusion), channel_id=1, replica_groups=mesh['rows'=32,'cols'=16] {'cols'}, dimensions={0} | all-to-all | bytes 524288 | tf_op jit(solution)/shard_map/all_to_all | solution.py:216
  76.1 0.6 copy.4
  (7 shorter events, 0.2 us)
Async XLA Ops:
  0.0 0.8 %copy-start.2 = (f32[4096]{0:T(1024)S(1)}, f32[4096]{0:T(1024)}, u32[]{:S(2)}) copy-start(f32[4096]{0:T(1024)} %param.2) | copy-start | bytes 49156
  0.0 0.7 slice-start.1
  25.1 1.0 %copy-start = (f32[17,8,512]{2,1,0:T(8,128)S(1)}, f32[17,8,512]{2,1,0:T(8,128)}, u32[]{:S(2)}) copy-start(f32[17,8,512]{2,1,0:T(8,128)} %shard_map.28) | copy-start | bytes 835588
  43.2 8.5 %copy-start.1 = (f32[136,512]{1,0:T(8,128)S(1)}, f32[136,512]{1,0:T(8,128)}, u32[]{:S(2)}) copy-start(f32[136,512]{1,0:T(8,128)} %shard_map.29) | copy-start | bytes 835588
  44.0 7.7 %collective-permute-start = (f32[8,512]{1,0:T(8,128)S(1)}, f32[8,512]{1,0:T(8,128)S(1)}, u32[]{:S(2)}, u32[]{:S(2)}) collective-permute-start(f32[8,512]{1,0:T(8,128)S(1)} %slice.45), channel_id=1, source_target_pairs={{0,16},{16,32},{32,48},{48,64},{64,80},{80,96},{96,112},{112,128},... | collective-permute-start | bytes 49160 | tf_op jit(solution)/shard_map/ppermute | solution.py:22
  47.1 4.7 %slice-start = ((f32[136,512]{1,0:T(8,128)}), f32[120,512]{1,0:T(8,128)S(1)}, s32[]{:S(2)}) async-start(f32[136,512]{1,0:T(8,128)} %shard_map.29), calls=%async_computation.1 | async-start | bytes 491520 | tf_op jit(solution)/shard_map/slice | solution.py:214

commit v3 on v2

--- a/solution.py
+++ b/solution.py
@@ -32,6 +32,19 @@
     return centre * factor
 
 
+def split_dot(a, b):
+    a_hi = a.astype(jnp.bfloat16)
+    b_hi = b.astype(jnp.bfloat16)
+    a_lo = (a - a_hi.astype(jnp.float32)).astype(jnp.bfloat16)
+    b_lo = (b - b_hi.astype(jnp.float32)).astype(jnp.bfloat16)
+    dims = (((1,), (1,)), ((), ()))
+
+    def dot(x, y):
+        return lax.dot_general(x, y, dims, preferred_element_type=jnp.float32)
+
+    return dot(a_hi, b_hi) + (dot(a_hi, b_lo) + dot(a_lo, b_hi))
+
+
 def tile_kernel(n_tiles, idx_ref, blocks_ref, out_ref):
     out_ref[...] = jnp.full(out_ref.shape, -1.0, jnp.float32)
     q = lax.broadcasted_iota(jnp.int32, (B, B), 0)
@@ -43,13 +56,7 @@
         j = i + d
         zl = windows(blocks_ref[pl.ds(i, 1), :])
         zr = windows(blocks_ref[pl.ds(j, 1), :])
-        corr = lax.dot_general(
-            zl,
-            zr,
-            (((1,), (1,)), ((), ())),
-            precision=lax.Precision.HIGHEST,
-            preferred_element_type=jnp.float32,
-        )
+        corr = split_dot(zl, zr)
         corr = jnp.where(d * B + s - q >= EXCL, corr, jnp.float32(-1.0))
         col_max = jnp.max(corr, axis=0, keepdims=True)
         row_max_c = jnp.max(corr, axis=1, keepdims=True)
@@ -73,7 +80,7 @@
         ],
         out_specs=pl.BlockSpec(memory_space=pltpu.VMEM),
         cost_estimate=pl.CostEstimate(
-            flops=n_tiles * 2 * B * B * M * 6,
+            flops=n_tiles * 2 * B * B * M * 3,
             bytes_accessed=n_blocks * (SEG + B) * 4,
             transcendentals=n_tiles * 2 * B,
         ),

time: 77.2 us -> 75.6 us (0.979)
  Pallas kernels: 34.6 us -> 33.1 us
    pallas_call x1, Pallas kernels: 12 us -> 10.5 us  [tile_maxima(): pl.pallas_call(lambda *refs: tile_kernel(n_tiles, *refs), out_shape=jax.S...]
where the time goes in v3:
time: 75.6 us; the launch traced here: 75.2 us
  Pallas kernels  33.1 us (44%)
  blocking collectives  24.3 us (32%)
  local copies, waits for them, and re-layouts  9.21 us (12%)
  waiting for transfers between devices  4.68 us (6%)
  starting transfers between devices  3.03 us (4%)
  other arithmetic  0.87 us (1%)
    all_to_all x1, blocking collectives, on_device(): got = lax.all_to_all(chunks, 'cols', 0, 0, tiled=True)  24.3 us
    pallas_call x1, Pallas kernels, gather_group(): pl.pallas_call(lambda *refs: gather_kernel(n_rows, n_cols, *refs), out_sh...  22.6 us
    pallas_call x1, Pallas kernels, tile_maxima(): pl.pallas_call(lambda *refs: tile_kernel(n_tiles, *refs), out_shape=jax.S...  10.5 us
    ppermute x1, waiting for transfers between devices, passed_along(): return lax.ppermute(block, axis, route)  4.68 us
    rev x1, local copies, waits for them, and re-layouts, on_device(): jnp.concatenate([by_block[:n_blocks], by_block[1:, :M]], axis=1)[:, ::-1]  4.37 us
    ppermute x1, starting transfers between devices, passed_along(): return lax.ppermute(block, axis, route)  3.03 us
    unnamed x8, local copies, waits for them, and re-layouts  2.57 us
  transfers between devices with their start and end apart: 1, of which 1 were waited for; matrix products, arithmetic and copies ran while one was open for 0% of the time, Pallas kernels for 0%

profile of v3, /device:TPU:64, one launch (start us, length us, event | category | flops | bytes accessed | tf_op | source)
XLA Modules:
  0.0 75.2 jit_solution(9370485987566633691)
XLA Ops:
  0.0 0.0 copy-start.2
  0.0 0.0 slice-start.1
  0.0 0.7 slice-done.1
  0.7 0.1 reshape.37
  0.8 0.0 copy-done.2
  0.8 0.6 reshape.38.refs_0_
  1.4 22.6 %shard_map.28 = f32[17,8,512]{2,1,0:T(8,128)} custom-call(f32[8,512]{1,0:T(8,128)} %reshape.38.refs_0_), custom_call_target="tpu_custom_call" | custom-call | tf_op jit(solution)/shard_map/pallas_call | solution.py:184
  24.0 1.0 %copy.3 = f32[17,4,8,128]{3,1,2,0:T(4,128)S(1)} copy(f32[17,4,8,128]{3,2,1,0:T(8,128)} %bitcast.9) | data formatting | bytes 557056
  25.1 0.0 copy-start
  25.1 0.9 %copy-done = f32[17,8,512]{2,1,0:T(8,128)S(1)} copy-done((f32[17,8,512]{2,1,0:T(8,128)S(1)}, f32[17,8,512]{2,1,0:T(8,128)}, u32[]{:S(2)}) %copy-start) | copy-done | bytes 278552
  26.1 4.4 %rev.3.refs_1_ = f32[136,768]{1,0:T(8,128)} reverse(f32[136,768]{1,0:T(8,128)S(1)} %pad_maximum_fusion), dimensions={1} | reverse | bytes 835584 | tf_op jit(solution)/shard_map/rev | solution.py:208
  30.4 0.2 fusion
  30.6 0.6 pad_add_fusion.refs_0_
  31.2 10.5 %shard_map.29 = f32[136,512]{1,0:T(8,128)} custom-call(s32[2,4]{1,0:T(2,128)} %pad_add_fusion.refs_0_, f32[136,768]{1,0:T(8,128)} %rev.3.refs_1_), custom_call_target="tpu_custom_call" | custom-call | flops 1610612736 | bytes 696320 | tf_op jit(solution)/shard_map/pallas_call | solution.py:74
  41.7 0.0 copy-start.1
  41.7 0.8 %slice.45 = f32[8,512]{1,0:T(8,128)S(1)} slice(f32[136,512]{1,0:T(8,128)} %shard_map.29), slice={[128:136], [0:512]} | slice | bytes 32768 | tf_op jit(solution)/shard_map/slice | solution.py:218
  42.5 3.0 %collective-permute-start = (f32[8,512]{1,0:T(8,128)S(1)}, f32[8,512]{1,0:T(8,128)S(1)}, u32[]{:S(2)}, u32[]{:S(2)}) collective-permute-start(f32[8,512]{1,0:T(8,128)S(1)} %slice.45), channel_id=1, source_target_pairs={{0,16},{16,32},{32,48},{48,64},{64,80},{80,96},{96,112},{112,128},... | collective-permute-start | bytes 49160 | tf_op jit(solution)/shard_map/ppermute | solution.py:22
  45.6 0.0 slice-start
  45.6 4.7 %collective-permute-done = f32[8,512]{1,0:T(8,128)S(1)} collective-permute-done((f32[8,512]{1,0:T(8,128)S(1)}, f32[8,512]{1,0:T(8,128)S(1)}, u32[]{:S(2)}, u32[]{:S(2)}) %collective-permute-start) | collective-permute-done | bytes 16416 | tf_op jit(solution)/shard_map/ppermute | solution.py:22
  50.2 0.0 copy-done.1
  50.3 0.0 slice-done
  50.3 24.3 %all_to_all.5 = f32[16,8,512]{2,1,0:T(8,128)S(1)} all-to-all(f32[16,8,512]{2,1,0:T(8,128)S(1)} %maximum_bitcast_fusion), channel_id=1, replica_groups=mesh['rows'=32,'cols'=16] {'cols'}, dimensions={0} | all-to-all | bytes 524288 | tf_op jit(solution)/shard_map/all_to_all | solution.py:223
  74.6 0.6 copy.4
  (7 shorter events, 0.2 us)
Async XLA Ops:
  0.0 0.8 %copy-start.2 = (f32[4096]{0:T(1024)S(1)}, f32[4096]{0:T(1024)}, u32[]{:S(2)}) copy-start(f32[4096]{0:T(1024)} %param.2) | copy-start | bytes 49156
  0.0 0.7 slice-start.1
  25.1 1.0 %copy-start = (f32[17,8,512]{2,1,0:T(8,128)S(1)}, f32[17,8,512]{2,1,0:T(8,128)}, u32[]{:S(2)}) copy-start(f32[17,8,512]{2,1,0:T(8,128)} %shard_map.28) | copy-start | bytes 835588
  41.7 8.5 %copy-start.1 = (f32[136,512]{1,0:T(8,128)S(1)}, f32[136,512]{1,0:T(8,128)}, u32[]{:S(2)}) copy-start(f32[136,512]{1,0:T(8,128)} %shard_map.29) | copy-start | bytes 835588
  42.5 7.7 %collective-permute-start = (f32[8,512]{1,0:T(8,128)S(1)}, f32[8,512]{1,0:T(8,128)S(1)}, u32[]{:S(2)}, u32[]{:S(2)}) collective-permute-start(f32[8,512]{1,0:T(8,128)S(1)} %slice.45), channel_id=1, source_target_pairs={{0,16},{16,32},{32,48},{48,64},{64,80},{80,96},{96,112},{112,128},... | collective-permute-start | bytes 49160 | tf_op jit(solution)/shard_map/ppermute | solution.py:22
  45.6 4.7 %slice-start = ((f32[136,512]{1,0:T(8,128)}), f32[120,512]{1,0:T(8,128)S(1)}, s32[]{:S(2)}) async-start(f32[136,512]{1,0:T(8,128)} %shard_map.29), calls=%async_computation.1 | async-start | bytes 491520 | tf_op jit(solution)/shard_map/slice | solution.py:221

commit v4 on v3

--- a/solution.py
+++ b/solution.py
@@ -91,90 +91,112 @@
     g = lax.axis_index("rows")
     c = lax.axis_index("cols")
     barrier = pltpu.get_barrier_semaphore()
-    for p in range(n_cols):
-        @pl.when(p != c)
+    half = (c // 2) % 2
+    peers = [p for p in range(n_cols)]
+    for p in peers:
+        @pl.when(jnp.logical_and(p != c, jnp.logical_or((p // 2) % 2 == half, p == c ^ 2)))
         def _():
             pl.semaphore_signal(barrier, 1, device_id=(g, p), device_id_type=MESH)
 
-    @pl.when(g + 1 < n_rows)
+    collector = jnp.logical_or(c == 0, c == 2)
+    up = jnp.logical_and(collector, g + 1 < n_rows)
+
+    @pl.when(up)
     def _():
         pl.semaphore_signal(barrier, 1, device_id=(g + 1, 0), device_id_type=MESH)
 
-    first = jnp.logical_and(c == 0, g > 0)
-
-    @pl.when(first)
-    def _():
-        for p in range(n_cols):
-            pl.semaphore_signal(barrier, 1, device_id=(g - 1, p), device_id_type=MESH)
-
-    count = (n_cols - 1) + (g + 1 < n_rows).astype(jnp.int32) + n_cols * first.astype(jnp.int32)
+    down = jnp.logical_and(c == 0, g > 0)
+
+    @pl.when(down)
+    def _():
+        pl.semaphore_signal(barrier, 1, device_id=(g - 1, 0), device_id_type=MESH)
+        pl.semaphore_signal(barrier, 1, device_id=(g - 1, 2), device_id_type=MESH)
+
+    count = n_cols // 2 + up.astype(jnp.int32) + 2 * down.astype(jnp.int32)
     pl.semaphore_wait(barrier, count)
-    return g, c, first
+    return g, c, half, collector, up, down
+
+
+def half_peers(n_cols, c, half):
+    return [
+        (p, jnp.logical_and(p != c, (p // 2) % 2 == half)) for p in range(n_cols)
+    ]
 
 
 def gather_kernel(n_rows, n_cols, piece_ref, out_ref, held, send_sems, recv_sems):
-    g, c, first = greet_partners(n_rows, n_cols)
-
-    def to_peer(p):
+    g, c, half, collector, up, down = greet_partners(n_rows, n_cols)
+    mate = c ^ 2
+    head = n_cols
+
+    def remote(src, slot, sem, device):
         return pltpu.make_async_remote_copy(
-            src_ref=piece_ref,
-            dst_ref=held.at[c],
-            send_sem=send_sems.at[p],
-            recv_sem=recv_sems.at[c],
-            device_id=(g, p),
+            src_ref=src,
+            dst_ref=held.at[slot],
+            send_sem=send_sems.at[sem],
+            recv_sem=recv_sems.at[slot],
+            device_id=device,
             device_id_type=MESH,
         )
 
-    def from_peer(p):
-        return pltpu.make_async_remote_copy(
-            src_ref=piece_ref,
-            dst_ref=held.at[p],
-            send_sem=send_sems.at[p],
-            recv_sem=recv_sems.at[p],
-            device_id=(g, p),
-            device_id_type=MESH,
-        )
-
-    def head_to(p):
-        return pltpu.make_async_remote_copy(
-            src_ref=piece_ref,
-            dst_ref=held.at[n_cols],
-            send_sem=send_sems.at[n_cols + p],
-            recv_sem=recv_sems.at[n_cols],
-            device_id=(g - 1, p),
-            device_id_type=MESH,
-        )
-
-    @pl.when(first)
-    def _():
-        for p in range(n_cols):
-            head_to(p).start()
-
-    for p in range(n_cols):
-        @pl.when(p != c)
-        def _():
-            to_peer(p).start()
+    to_mate = remote(piece_ref, c, 0, (g, mate))
+    to_mate.start()
+
+    @pl.when(down)
+    def _():
+        remote(piece_ref, head, 1, (g - 1, 0)).start()
+        remote(piece_ref, head, 2, (g - 1, 2)).start()
+
+    @pl.when(g + 1 == n_rows)
+    def _():
+        held[head] = jnp.zeros(piece_ref.shape, jnp.float32)
+
+    remote(piece_ref, mate, 0, (g, mate)).wait_recv()
+
+    @pl.when(up)
+    def _():
+        remote(piece_ref, head, 1, (g + 1, 0)).wait_recv()
+
+    peers = half_peers(n_cols, c, half)
+    for p, live in peers:
+        @pl.when(live)
+        def _():
+            remote(piece_ref, c, 3 + 3 * p, (g, p)).start()
+            remote(held.at[mate], mate, 4 + 3 * p, (g, p)).start()
+
+        @pl.when(jnp.logical_and(live, up))
+        def _():
+            remote(held.at[head], head, 5 + 3 * p, (g, p)).start()
 
     held[pl.ds(c, 1)] = piece_ref[...][None]
 
-    @pl.when(g + 1 == n_rows)
-    def _():
-        held[n_cols] = jnp.zeros(piece_ref.shape, jnp.float32)
-
-    for p in range(n_cols):
-        @pl.when(p != c)
-        def _():
-            from_peer(p).wait_recv()
-            to_peer(p).wait_send()
-
-    @pl.when(g + 1 < n_rows)
-    def _():
-        head_to(0).wait_recv()
-
-    @pl.when(first)
-    def _():
-        for p in range(n_cols):
-            head_to(p).wait_send()
+    for p, live in peers:
+        @pl.when(live)
+        def _():
+            remote(piece_ref, p, 3 + 3 * p, (g, p)).wait_recv()
+            remote(piece_ref, p ^ 2, 3 + 3 * p, (g, p)).wait_recv()
+
+    not_collector = jnp.logical_and(jnp.logical_not(collector), g + 1 < n_rows)
+
+    @pl.when(not_collector)
+    def _():
+        remote(piece_ref, head, 1, (g, 0)).wait_recv()
+
+    to_mate.wait_send()
+
+    @pl.when(down)
+    def _():
+        remote(piece_ref, head, 1, (g - 1, 0)).wait_send()
+        remote(piece_ref, head, 2, (g - 1, 2)).wait_send()
+
+    for p, live in peers:
+        @pl.when(live)
+        def _():
+            remote(piece_ref, c, 3 + 3 * p, (g, p)).wait_send()
+            remote(piece_ref, c, 4 + 3 * p, (g, p)).wait_send()
+
+        @pl.when(jnp.logical_and(live, up))
+        def _():
+            remote(piece_ref, c, 5 + 3 * p, (g, p)).wait_send()
 
     out_ref[...] = held[...]
 
@@ -188,11 +210,125 @@
         out_specs=pl.BlockSpec(memory_space=pltpu.VMEM),
         scratch_shapes=[
             pltpu.VMEM(shape, jnp.float32),
-            pltpu.SemaphoreType.DMA((2 * n_cols,)),
+            pltpu.SemaphoreType.DMA((3 + 3 * n_cols,)),
             pltpu.SemaphoreType.DMA((n_cols + 1,)),
         ],
         compiler_params=pltpu.CompilerParams(collective_id=0, has_side_effects=True),
     )(piece)
+
+
+def reduce_kernel(n_rows, n_cols, part_ref, out_ref, got, mine, spills, send_sems, recv_sems):
+    got[...] = jnp.full(got.shape, -1.0, jnp.float32)
+    spills[...] = jnp.full(spills.shape, -1.0, jnp.float32)
+    g, c, half, collector, up, down = greet_partners(n_rows, n_cols)
+    mate = c ^ 2
+    spill = n_cols
+    hub = 2 * half
+    peers = half_peers(n_cols, c, half)
+
+    def remote(src, dst, send, recv, device):
+        return pltpu.make_async_remote_copy(
+            src_ref=src,
+            dst_ref=dst,
+            send_sem=send_sems.at[send],
+            recv_sem=recv_sems.at[recv],
+            device_id=device,
+            device_id_type=MESH,
+        )
+
+    def to_peer(p, k):
+        return remote(part_ref.at[p ^ (2 * k)], got.at[c, k], 3 * p + k, 2 * c + k, (g, p))
+
+    def from_peer(p, k):
+        return remote(part_ref.at[p], got.at[p, k], 3 * p + k, 2 * p + k, (g, p))
+
+    def spill_to_hub():
+        return remote(part_ref.at[spill], got.at[c, 2], 3 * n_cols, 2 * n_cols + 1 + c, (g, hub))
+
+    def spill_from(p):
+        return remote(part_ref.at[spill], got.at[p, 2], 3 * n_cols, 2 * n_cols + 1 + p, (g, p))
+
+    for p, live in peers:
+        @pl.when(live)
+        def _():
+            to_peer(p, 0).start()
+            to_peer(p, 1).start()
+
+    @pl.when(jnp.logical_not(collector))
+    def _():
+        spill_to_hub().start()
+
+    for p, live in peers:
+        @pl.when(live)
+        def _():
+            from_peer(p, 0).wait_recv()
+            from_peer(p, 1).wait_recv()
+
+    acc = jnp.maximum(part_ref[pl.ds(c, 1)][0], jnp.max(got[:, 0], axis=0))
+    mine[0] = jnp.maximum(part_ref[pl.ds(mate, 1)][0], jnp.max(got[:, 1], axis=0))
+
+    to_mate = remote(mine.at[0], mine.at[1], 3 * n_cols + 1, 3 * n_cols + 1, (g, mate))
+    to_mate.start()
+
+    @pl.when(collector)
+    def _():
+        for p, live in peers:
+            @pl.when(live)
+            def _():
+                spill_from(p).wait_recv()
+
+    mine[2] = jnp.maximum(part_ref[spill], jnp.max(got[:, 2], axis=0))
+
+    def spill_up():
+        return remote(mine.at[2], spills.at[half], 3 * n_cols + 2, 3 * n_cols + 2 + half, (g + 1, 0))
+
+    @pl.when(up)
+    def _():
+        spill_up().start()
+
+    to_mate.wait_recv()
+
+    @pl.when(down)
+    def _():
+        remote(mine.at[2], spills.at[0], 3 * n_cols + 2, 3 * n_cols + 2, (g - 1, 0)).wait_recv()
+        remote(mine.at[2], spills.at[1], 3 * n_cols + 2, 3 * n_cols + 3, (g - 1, 2)).wait_recv()
+
+    acc = jnp.maximum(acc, mine[1])
+    out_ref[...] = jnp.maximum(acc, jnp.maximum(spills[0], spills[1]))
+
+    for p, live in peers:
+        @pl.when(live)
+        def _():
+            to_peer(p, 0).wait_send()
+            to_peer(p, 1).wait_send()
+
+    @pl.when(jnp.logical_not(collector))
+    def _():
+        spill_to_hub().wait_send()
+
+    to_mate.wait_send()
+
+    @pl.when(up)
+    def _():
+        spill_up().wait_send()
+
+
+def reduce_group(partial, n_rows, n_cols):
+    chunk = partial.shape[1:]
+    return pl.pallas_call(
+        lambda *refs: reduce_kernel(n_rows, n_cols, *refs),
+        out_shape=jax.ShapeDtypeStruct(chunk, jnp.float32),
+        in_specs=[pl.BlockSpec(memory_space=pltpu.VMEM)],
+        out_specs=pl.BlockSpec(memory_space=pltpu.VMEM),
+        scratch_shapes=[
+            pltpu.VMEM((n_cols, 3) + chunk, jnp.float32),
+            pltpu.VMEM((3,) + chunk, jnp.float32),
+            pltpu.VMEM((2,) + chunk, jnp.float32),
+            pltpu.SemaphoreType.DMA((3 * n_cols + 3,)),
+            pltpu.SemaphoreType.DMA((3 * n_cols + 4,)),
+        ],
+        compiler_params=pltpu.CompilerParams(collective_id=1, has_side_effects=True),
+    )(partial)
 
 
 def on_device(series, tile_list):
@@ -214,14 +350,7 @@
     idx = jnp.stack([mine[0] - group * BPR, mine[1]])
 
     partial = tile_maxima(idx, blocks)
-    own = partial[:BPR]
-    spill = partial[BPR:]
-    arrived = passed_along(spill, "rows", 1)
-    arrived = jnp.where(group > 0, arrived, jnp.float32(-1.0))
-    own = jnp.concatenate([jnp.maximum(own[:SPILL], arrived), own[SPILL:]])
-    chunks = own.reshape(col_count, BPR // col_count, B)
-    got = lax.all_to_all(chunks, "cols", 0, 0, tiled=True)
-    result = jnp.max(got.reshape(col_count, BPR // col_count, B), axis=0)
+    result = reduce_group(partial.reshape(col_count + 1, SPILL, B), n_rows, col_count)
     return result.reshape(piece)
 
 

time: 75.6 us -> 60.3 us (0.80)
  blocking collectives: 24.3 us -> 0 us
  Pallas kernels: 33.1 us -> 50 us
  waiting for transfers between devices: 4.68 us -> 0 us
  starting transfers between devices: 3.03 us -> 0 us
    all_to_all x1 -> x0, blocking collectives: 24.3 us -> none  [on_device(): got = lax.all_to_all(chunks, 'cols', 0, 0, tiled=True)]
    pallas_call x0 -> x1, Pallas kernels: none -> 20.1 us  [reduce_group(): pl.pallas_call(lambda *refs: reduce_kernel(n_rows, n_cols, *refs), out_sh...]
    ppermute x1 -> x0, waiting for transfers between devices: 4.68 us -> none  [passed_along(): return lax.ppermute(block, axis, route)]
    pallas_call x1, Pallas kernels: 22.6 us -> 19.4 us  [gather_group(): pl.pallas_call(lambda *refs: gather_kernel(n_rows, n_cols, *refs), out_sh...]
    ppermute x1 -> x0, starting transfers between devices: 3.03 us -> none  [passed_along(): return lax.ppermute(block, axis, route)]
    slice x3 -> x0, local copies, waits for them, and re-layouts: 0.8 us -> none  [the longest x1 0.79 us: on_device(): spill = partial[BPR:]]
    unnamed x8 -> x6, local copies, waits for them, and re-layouts: 2.57 us -> 3.29 us
  transfers between devices with their start and end apart: 1 -> 0, of which waited for: 1 -> 0; matrix products, arithmetic and copies ran while one was open for 0% -> 0% of each run, Pallas kernels for 0% -> 0%
where the time goes in v4:
time: 60.3 us; the launch traced here: 59.9 us
  Pallas kernels  50 us (83%)
  local copies, waits for them, and re-layouts  9.09 us (15%)
  other arithmetic  0.81 us (1%)
    pallas_call x1, Pallas kernels, reduce_group(): pl.pallas_call(lambda *refs: reduce_kernel(n_rows, n_cols, *refs), out_sh...  20.1 us
    pallas_call x1, Pallas kernels, gather_group(): pl.pallas_call(lambda *refs: gather_kernel(n_rows, n_cols, *refs), out_sh...  19.4 us
    pallas_call x1, Pallas kernels, tile_maxima(): pl.pallas_call(lambda *refs: tile_kernel(n_tiles, *refs), out_shape=jax.S...  10.5 us
    rev x1, local copies, waits for them, and re-layouts, on_device(): jnp.concatenate([by_block[:n_blocks], by_block[1:, :M]], axis=1)[:, ::-1]  4.36 us
    unnamed x6, local copies, waits for them, and re-layouts  3.29 us

profile of v4, /device:TPU:64, one launch (start us, length us, event | category | flops | bytes accessed | tf_op | source)
XLA Modules:
  0.0 59.9 jit_solution(6996609217591133304)
XLA Ops:
  0.0 0.0 slice-start
  0.0 0.0 copy-start.1
  0.0 0.7 %slice-done = s32[2,64]{1,0:T(2,128)S(1)} async-done(((s32[3,64]{1,0:T(4,128)}), s32[2,64]{1,0:T(2,128)S(1)}, s32[]{:S(2)}) %slice-start) | async-done | bytes 536 | tf_op jit(solution)/shard_map/slice | solution.py:348
  0.7 0.1 reshape.37
  0.8 0.2 fusion
  1.0 0.6 pad_add_fusion.refs_0_
  1.5 0.0 copy-done.1
  1.5 0.6 %reshape.38.refs_0_ = f32[8,512]{1,0:T(8,128)} reshape(f32[4096]{0:T(1024)S(1)} %copy-done.1) | data formatting | bytes 32768 | tf_op jit(solution)/shard_map/reshape | solution.py:340
  2.2 19.4 %shard_map.28 = f32[17,8,512]{2,1,0:T(8,128)} custom-call(f32[8,512]{1,0:T(8,128)} %reshape.38.refs_0_), custom_call_target="tpu_custom_call" | custom-call | tf_op jit(solution)/shard_map/pallas_call | solution.py:206
  21.6 1.0 %copy.3 = f32[17,4,8,128]{3,1,2,0:T(4,128)S(1)} copy(f32[17,4,8,128]{3,2,1,0:T(8,128)} %bitcast.8) | data formatting | bytes 557056
  22.7 0.0 copy-start
  22.7 0.9 %copy-done = f32[17,8,512]{2,1,0:T(8,128)S(1)} copy-done((f32[17,8,512]{2,1,0:T(8,128)S(1)}, f32[17,8,512]{2,1,0:T(8,128)}, u32[]{:S(2)}) %copy-start) | copy-done | bytes 278552
  23.7 4.4 %rev.3.refs_1_ = f32[136,768]{1,0:T(8,128)} reverse(f32[136,768]{1,0:T(8,128)S(1)} %pad_maximum_fusion), dimensions={1} | reverse | bytes 835584 | tf_op jit(solution)/shard_map/rev | solution.py:344
  28.0 10.5 %shard_map.29 = f32[136,512]{1,0:T(8,128)} custom-call(s32[2,4]{1,0:T(2,128)} %pad_add_fusion.refs_0_, f32[136,768]{1,0:T(8,128)} %rev.3.refs_1_), custom_call_target="tpu_custom_call" | custom-call | flops 1610612736 | bytes 696320 | tf_op jit(solution)/shard_map/pallas_call | solution.py:74
  38.5 20.1 %shard_map.30 = f32[8,512]{1,0:T(8,128)} custom-call(f32[17,8,512]{2,1,0:T(8,128)} %bitcast.11), custom_call_target="tpu_custom_call" | custom-call | tf_op jit(solution)/shard_map/pallas_call | solution.py:318
  58.6 1.3 %copy.4 = f32[1,4,8,128]{3,1,2,0:T(4,128)} copy(f32[1,4,8,128]{3,2,1,0:T(8,128)} %bitcast.12) | data formatting | bytes 32768
  (4 shorter events, 0.1 us)
Async XLA Ops:
  0.0 0.7 %slice-start = ((s32[3,64]{1,0:T(4,128)}), s32[2,64]{1,0:T(2,128)S(1)}, s32[]{:S(2)}) async-start(s32[3,64]{1,0:T(4,128)} %param.3), calls=%async_computation | async-start | bytes 2048 | tf_op jit(solution)/shard_map/slice | solution.py:348
  0.0 1.5 %copy-start.1 = (f32[4096]{0:T(1024)S(1)}, f32[4096]{0:T(1024)}, u32[]{:S(2)}) copy-start(f32[4096]{0:T(1024)} %param.2) | copy-start | bytes 49156
  22.7 1.0 %copy-start = (f32[17,8,512]{2,1,0:T(8,128)S(1)}, f32[17,8,512]{2,1,0:T(8,128)}, u32[]{:S(2)}) copy-start(f32[17,8,512]{2,1,0:T(8,128)} %shard_map.28) | copy-start | bytes 835588

commit v5 on v4

v5 whole, which is shorter than its diff:
```python
import math

import jax
import jax.numpy as jnp
from jax import lax
from jax.experimental import pallas as pl
from jax.experimental.pallas import tpu as pltpu
from jax.sharding import PartitionSpec as P

M = 256
B = 512
BPR = 128
EXCL = 64
SPILL = 8
SEG = B + M
MESH = pl.DeviceIdType.MESH


def passed_along(block, axis, distance):
    devices = range(lax.axis_size(axis))
    route = [(i - distance, i) for i in devices if i - distance in devices]
    return lax.ppermute(block, axis, route)


def windows(held, b):
    seg = jnp.concatenate([held[pl.ds(b, 1), :], held[pl.ds(b + 1, 1), :][:, :M]], axis=1)
    wide = jnp.broadcast_to(seg, (B, SEG))
    rolled = pltpu.roll(wide, 1, 1, stride=1, stride_axis=0)
    w = rolled[:, B:SEG]
    centre = w - jnp.mean(w, axis=1, keepdims=True)
    spread = jnp.mean(centre * centre, axis=1, keepdims=True)
    factor = lax.rsqrt(spread + 1e-05) / math.sqrt(M)
    return centre * factor


def split_dot(a, b):
    a_hi = a.astype(jnp.bfloat16)
    b_hi = b.astype(jnp.bfloat16)
    a_lo = (a - a_hi.astype(jnp.float32)).astype(jnp.bfloat16)
    b_lo = (b - b_hi.astype(jnp.float32)).astype(jnp.bfloat16)
    dims = (((1,), (1,)), ((), ()))

    def dot(x, y):
        return lax.dot_general(x, y, dims, preferred_element_type=jnp.float32)

    return dot(a_hi, b_hi) + (dot(a_hi, b_lo) + dot(a_lo, b_hi))


def greet_partners(n_rows, n_cols):
    g = lax.axis_index("rows")
    c = lax.axis_index("cols")
    barrier = pltpu.get_barrier_semaphore()
    half = (c // 2) % 2
    peers = [p for p in range(n_cols)]
    for p in peers:
        @pl.when(jnp.logical_and(p != c, jnp.logical_or((p // 2) % 2 == half, p == c ^ 2)))
        def _():
            pl.semaphore_signal(barrier, 1, device_id=(g, p), device_id_type=MESH)

    collector = jnp.logical_or(c == 0, c == 2)
    up = jnp.logical_and(collector, g + 1 < n_rows)

    @pl.when(up)
    def _():
        pl.semaphore_signal(barrier, 1, device_id=(g + 1, 0), device_id_type=MESH)

    down = jnp.logical_and(c == 0, g > 0)

    @pl.when(down)
    def _():
        pl.semaphore_signal(barrier, 1, device_id=(g - 1, 0), device_id_type=MESH)
        pl.semaphore_signal(barrier, 1, device_id=(g - 1, 2), device_id_type=MESH)

    count = n_cols // 2 + up.astype(jnp.int32) + 2 * down.astype(jnp.int32)
    pl.semaphore_wait(barrier, count)
    return g, c, half, collector, up, down


def half_peers(n_cols, c, half):
    return [
        (p, jnp.logical_and(p != c, (p // 2) % 2 == half)) for p in range(n_cols)
    ]


def fused_kernel(n_rows, n_cols, n_tiles, idx_ref, piece_ref, out_ref,
                 held, partial, got, mine, spills, g_send, g_recv, r_send, r_recv):
    got[...] = jnp.full(got.shape, -1.0, jnp.float32)
    spills[...] = jnp.full(spills.shape, -1.0, jnp.float32)
    partial[...] = jnp.full(partial.shape, -1.0, jnp.float32)
    g, c, half, collector, up, down = greet_partners(n_rows, n_cols)
    mate = c ^ 2
    head = n_cols
    rows = SPILL
    peers = half_peers(n_cols, c, half)

    def slab(ref, k):
        if isinstance(k, int):
            return ref.at[pl.ds(k * rows, rows)]
        return ref.at[pl.ds(pl.multiple_of(k * rows, rows), rows)]

    def remote(src, slot, sem, device):
        return pltpu.make_async_remote_copy(
            src_ref=src,
            dst_ref=slab(held, slot),
            send_sem=g_send.at[sem],
            recv_sem=g_recv.at[slot],
            device_id=device,
            device_id_type=MESH,
        )

    to_mate = remote(piece_ref, c, 0, (g, mate))
    to_mate.start()

    @pl.when(down)
    def _():
        remote(piece_ref, head, 1, (g - 1, 0)).start()
        remote(piece_ref, head, 2, (g - 1, 2)).start()

    @pl.when(g + 1 == n_rows)
    def _():
        held[pl.ds(head * rows, rows), :] = jnp.zeros(piece_ref.shape, jnp.float32)

    remote(piece_ref, mate, 0, (g, mate)).wait_recv()

    @pl.when(up)
    def _():
        remote(piece_ref, head, 1, (g + 1, 0)).wait_recv()

    for p, live in peers:
        @pl.when(live)
        def _():
            remote(piece_ref, c, 3 + 3 * p, (g, p)).start()
            remote(slab(held, mate), mate, 4 + 3 * p, (g, p)).start()

        @pl.when(jnp.logical_and(live, up))
        def _():
            remote(slab(held, head), head, 5 + 3 * p, (g, p)).start()

    held[pl.ds(pl.multiple_of(c * rows, rows), rows), :] = piece_ref[...]

    for p, live in peers:
        @pl.when(live)
        def _():
            remote(piece_ref, p, 3 + 3 * p, (g, p)).wait_recv()
            remote(piece_ref, p ^ 2, 3 + 3 * p, (g, p)).wait_recv()

    @pl.when(jnp.logical_and(jnp.logical_not(collector), g + 1 < n_rows))
    def _():
        remote(piece_ref, head, 1, (g, 0)).wait_recv()

    r_i = lax.broadcasted_iota(jnp.int32, (B, B), 0)
    r_j = lax.broadcasted_iota(jnp.int32, (B, B), 1)
    flip = r_i + r_j == B - 1

    def body(t, carry):
        i = idx_ref[0, t]
        d = idx_ref[1, t]
        j = i + d
        zl = windows(held, i)
        zr = windows(held, j)
        corr = split_dot(zl, zr)
        corr = jnp.where(d * B + r_i - r_j >= EXCL, corr, jnp.float32(-1.0))
        row_c = jnp.max(corr, axis=1, keepdims=True)
        row_max = jnp.sum(jnp.where(flip, row_c, 0.0), axis=0, keepdims=True)
        col_r = jnp.max(corr, axis=0, keepdims=True)
        col_c = jnp.sum(jnp.where(flip, col_r, 0.0), axis=1, keepdims=True)
        col_max = jnp.sum(jnp.where(r_i == r_j, col_c, 0.0), axis=0, keepdims=True)
        blk = lax.broadcasted_iota(jnp.int32, partial.shape, 0)
        upd = jnp.maximum(
            jnp.where(blk == i, row_max, jnp.float32(-1.0)),
            jnp.where(blk == j, col_max, jnp.float32(-1.0)),
        )
        partial[...] = jnp.maximum(partial[...], upd)
        return carry

    lax.fori_loop(0, n_tiles, body, 0)

    spill = n_cols

    def rremote(src, dst, send, recv, device):
        return pltpu.make_async_remote_copy(
            src_ref=src,
            dst_ref=dst,
            send_sem=r_send.at[send],
            recv_sem=r_recv.at[recv],
            device_id=device,
            device_id_type=MESH,
        )

    hub = 2 * half

    def to_peer(p, k):
        return rremote(slab(partial, p ^ (2 * k)), got.at[c, k], 3 * p + k, 2 * c + k, (g, p))

    def from_peer(p, k):
        return rremote(slab(partial, p), got.at[p, k], 3 * p + k, 2 * p + k, (g, p))

    def spill_to_hub():
        return rremote(slab(partial, spill), got.at[c, 2], 3 * n_cols, 2 * n_cols + 1 + c, (g, hub))

    def spill_from(p):
        return rremote(slab(partial, spill), got.at[p, 2], 3 * n_cols, 2 * n_cols + 1 + p, (g, p))

    for p, live in peers:
        @pl.when(live)
        def _():
            to_peer(p, 0).start()
            to_peer(p, 1).start()

    @pl.when(jnp.logical_not(collector))
    def _():
        spill_to_hub().start()

    for p, live in peers:
        @pl.when(live)
        def _():
            from_peer(p, 0).wait_recv()
            from_peer(p, 1).wait_recv()

    own = partial[pl.ds(pl.multiple_of(c * rows, rows), rows), :]
    mate_part = partial[pl.ds(pl.multiple_of(mate * rows, rows), rows), :]
    acc = jnp.maximum(own, jnp.max(got[:, 0], axis=0))
    mine[0] = jnp.maximum(mate_part, jnp.max(got[:, 1], axis=0))

    to_mate_r = rremote(mine.at[0], mine.at[1], 3 * n_cols + 1, 3 * n_cols + 1, (g, mate))
    to_mate_r.start()

    @pl.when(collector)
    def _():
        for p, live in peers:
            @pl.when(live)
            def _():
                spill_from(p).wait_recv()

    mine[2] = jnp.maximum(partial[pl.ds(spill * rows, rows), :], jnp.max(got[:, 2], axis=0))

    def spill_up():
        return rremote(mine.at[2], spills.at[half], 3 * n_cols + 2, 3 * n_cols + 2 + half, (g + 1, 0))

    @pl.when(up)
    def _():
        spill_up().start()

    to_mate_r.wait_recv()

    @pl.when(down)
    def _():
        rremote(mine.at[2], spills.at[0], 3 * n_cols + 2, 3 * n_cols + 2, (g - 1, 0)).wait_recv()
        rremote(mine.at[2], spills.at[1], 3 * n_cols + 2, 3 * n_cols + 3, (g - 1, 2)).wait_recv()

    acc = jnp.maximum(acc, mine[1])
    out_ref[...] = jnp.maximum(acc, jnp.maximum(spills[0], spills[1]))

    to_mate.wait_send()

    @pl.when(down)
    def _():
        remote(piece_ref, head, 1, (g - 1, 0)).wait_send()
        remote(piece_ref, head, 2, (g - 1, 2)).wait_send()

    for p, live in peers:
        @pl.when(live)
        def _():
            remote(piece_ref, c, 3 + 3 * p, (g, p)).wait_send()
            remote(piece_ref, c, 4 + 3 * p, (g, p)).wait_send()
            to_peer(p, 0).wait_send()
            to_peer(p, 1).wait_send()

        @pl.when(jnp.logical_and(live, up))
        def _():
            remote(piece_ref, c, 5 + 3 * p, (g, p)).wait_send()

    @pl.when(jnp.logical_not(collector))
    def _():
        spill_to_hub().wait_send()

    to_mate_r.wait_send()

    @pl.when(up)
    def _():
        spill_up().wait_send()


def fused_call(idx, piece, n_rows, n_cols):
    n_tiles = idx.shape[1]
    slots = n_cols + 1
    chunk = piece.shape
    return pl.pallas_call(
        lambda *refs: fused_kernel(n_rows, n_cols, n_tiles, *refs),
        out_shape=jax.ShapeDtypeStruct(chunk, jnp.float32),
        in_specs=[
            pl.BlockSpec(memory_space=pltpu.SMEM),
            pl.BlockSpec(memory_space=pltpu.VMEM),
        ],
        out_specs=pl.BlockSpec(memory_space=pltpu.VMEM),
        scratch_shapes=[
            pltpu.VMEM((slots * chunk[0], B), jnp.float32),
            pltpu.VMEM((slots * chunk[0], B), jnp.float32),
            pltpu.VMEM((n_cols, 3) + chunk, jnp.float32),
            pltpu.VMEM((3,) + chunk, jnp.float32),
            pltpu.VMEM((2,) + chunk, jnp.float32),
            pltpu.SemaphoreType.DMA((3 + 3 * n_cols,)),
            pltpu.SemaphoreType.DMA((slots,)),
            pltpu.SemaphoreType.DMA((3 * n_cols + 3,)),
            pltpu.SemaphoreType.DMA((3 * n_cols + 4,)),
        ],
        cost_estimate=pl.CostEstimate(
            flops=n_tiles * 2 * B * B * M * 3,
            bytes_accessed=slots * chunk[0] * B * 4,
            transcendentals=n_tiles * 2 * B,
        ),
        compiler_params=pltpu.CompilerParams(collective_id=0, has_side_effects=True),
    )(idx, piece)


def on_device(series, tile_list):
    piece = series.shape[0]
    col_count = lax.axis_size("cols")
    n_rows = lax.axis_size("rows")
    group = lax.axis_index("rows")
    col_id = lax.axis_index("cols")
    per_dev = tile_list.shape[1] // col_count
    mine = lax.dynamic_slice_in_dim(
        tile_list[:2].reshape(2, per_dev, col_count), col_id, 1, axis=2
    )[:, :, 0]
    idx = jnp.stack([mine[0] - group * BPR, mine[1]])
    result = fused_call(idx, series.reshape(SPILL, B), n_rows, col_count)
    return result.reshape(piece)


def solution(mesh):
    in_specs = (P(("rows", "cols")), P(None, "rows"))
    out_specs = P(("rows", "cols"))
    return jax.shard_map(
        on_device, mesh=mesh, in_specs=in_specs, out_specs=out_specs, check_vma=False
    )
```

time: 60.3 us -> 49.4 us (0.82)
  local copies, waits for them, and re-layouts: 9.09 us -> 2.7 us
  Pallas kernels: 50 us -> 45.6 us
    pallas_call x3 -> x1, Pallas kernels: 50 us -> 45.6 us  [fused_call(): pl.pallas_call(lambda *refs: fused_kernel(n_rows, n_cols, n_tiles, *refs)...]
    rev x1 -> x0, local copies, waits for them, and re-layouts: 4.36 us -> none  [on_device(): jnp.concatenate([by_block[:n_blocks], by_block[1:, :M]], axis=1)[:, ::-1]]
    unnamed x6 -> x3, local copies, waits for them, and re-layouts: 3.29 us -> 1.33 us
where the time goes in v5:
time: 49.4 us; the launch traced here: 49.1 us
  Pallas kernels  45.6 us (92%)
  local copies, waits for them, and re-layouts  2.7 us (5%)
  other arithmetic  0.81 us (2%)
    pallas_call x1, Pallas kernels, fused_call(): pl.pallas_call(lambda *refs: fused_kernel(n_rows, n_cols, n_tiles, *refs)...  45.6 us
    unnamed x3, local copies, waits for them, and re-layouts  1.33 us

profile of v5, /device:TPU:64, one launch (start us, length us, event | category | flops | bytes accessed | tf_op | source)
XLA Modules:
  0.0 49.1 jit_solution(8092875599114277380)
XLA Ops:
  0.0 0.0 slice-start
  0.0 0.0 copy-start
  0.0 0.7 %slice-done = s32[2,64]{1,0:T(2,128)S(1)} async-done(((s32[3,64]{1,0:T(4,128)}), s32[2,64]{1,0:T(2,128)S(1)}, s32[]{:S(2)}) %slice-start) | async-done | bytes 536 | tf_op jit(solution)/shard_map/slice | solution.py:324
  0.7 0.1 reshape.24
  0.8 0.2 fusion
  1.0 0.6 %pad_add_fusion.refs_0_ = s32[2,4]{1,0:T(2,128)} fusion(s32[1,4]{1,0:T(1,128)S(1)} %bitcast.6, s32[1,4]{1,0:T(1,128)S(1)} %bitcast.5), kind=kLoop, calls=%fused_computation.3 | loop fusion | flops 8 | bytes 64 | tf_op jit(solution)/shard_map/stack | solution.py:326
  1.6 0.0 copy-done
  1.6 0.6 %reshape.25.refs_1_ = f32[8,512]{1,0:T(8,128)} reshape(f32[4096]{0:T(1024)S(1)} %copy-done) | data formatting | bytes 32768 | tf_op jit(solution)/shard_map/reshape | solution.py:327
  2.2 45.6 %shard_map.28 = f32[8,512]{1,0:T(8,128)} custom-call(s32[2,4]{1,0:T(2,128)} %pad_add_fusion.refs_0_, f32[8,512]{1,0:T(8,128)} %reshape.25.refs_1_), custom_call_target="tpu_custom_call" | custom-call | flops 1610612736 | bytes 278528 | tf_op jit(solution)/shard_map/pallas_call | solution.py:288
  47.8 1.3 %copy.3 = f32[1,4,8,128]{3,1,2,0:T(4,128)} copy(f32[1,4,8,128]{3,2,1,0:T(8,128)} %bitcast.4) | data formatting | bytes 32768
Async XLA Ops:
  0.0 0.7 %slice-start = ((s32[3,64]{1,0:T(4,128)}), s32[2,64]{1,0:T(2,128)S(1)}, s32[]{:S(2)}) async-start(s32[3,64]{1,0:T(4,128)} %param.3), calls=%async_computation | async-start | bytes 2048 | tf_op jit(solution)/shard_map/slice | solution.py:324
  0.0 1.6 %copy-start = (f32[4096]{0:T(1024)S(1)}, f32[4096]{0:T(1024)}, u32[]{:S(2)}) copy-start(f32[4096]{0:T(1024)} %param.2) | copy-start | bytes 49156

commit v6 on v5

--- a/solution.py
+++ b/solution.py
@@ -24,9 +24,12 @@
 
 def windows(held, b):
     seg = jnp.concatenate([held[pl.ds(b, 1), :], held[pl.ds(b + 1, 1), :][:, :M]], axis=1)
-    wide = jnp.broadcast_to(seg, (B, SEG))
-    rolled = pltpu.roll(wide, 1, 1, stride=1, stride_axis=0)
-    w = rolled[:, B:SEG]
+    parts = []
+    for m in range(B // 128):
+        lo = 3 * 128 - 128 * m
+        sub = jnp.broadcast_to(seg[:, lo:lo + 3 * 128], (128, 3 * 128))
+        parts.append(pltpu.roll(sub, 1, 1, stride=1, stride_axis=0)[:, 128:])
+    w = jnp.concatenate(parts, axis=0)
     centre = w - jnp.mean(w, axis=1, keepdims=True)
     spread = jnp.mean(centre * centre, axis=1, keepdims=True)
     factor = lax.rsqrt(spread + 1e-05) / math.sqrt(M)
@@ -82,7 +85,7 @@
     ]
 
 
-def fused_kernel(n_rows, n_cols, n_tiles, idx_ref, piece_ref, out_ref,
+def fused_kernel(n_rows, n_cols, n_tiles, tiles_ref, piece_ref, out_ref,
                  held, partial, got, mine, spills, g_send, g_recv, r_send, r_recv):
     got[...] = jnp.full(got.shape, -1.0, jnp.float32)
     spills[...] = jnp.full(spills.shape, -1.0, jnp.float32)
@@ -153,8 +156,9 @@
     flip = r_i + r_j == B - 1
 
     def body(t, carry):
-        i = idx_ref[0, t]
-        d = idx_ref[1, t]
+        col = c + n_cols * t
+        i = jnp.clip(tiles_ref[0, col] - g * BPR, 0, BPR - 1)
+        d = jnp.clip(tiles_ref[1, col], 0, SPILL - 1)
         j = i + d
         zl = windows(held, i)
         zr = windows(held, j)
@@ -249,7 +253,12 @@
         rremote(mine.at[2], spills.at[1], 3 * n_cols + 2, 3 * n_cols + 3, (g - 1, 2)).wait_recv()
 
     acc = jnp.maximum(acc, mine[1])
-    out_ref[...] = jnp.maximum(acc, jnp.maximum(spills[0], spills[1]))
+    acc = jnp.maximum(acc, jnp.maximum(spills[0], spills[1]))
+    lanes = 128
+    per_row = B // lanes
+    for k in range(rows):
+        for v in range(per_row):
+            out_ref[pl.ds(k * per_row + v, 1), :] = acc[k:k + 1, v * lanes:(v + 1) * lanes]
 
     to_mate.wait_send()
 
@@ -281,13 +290,13 @@
         spill_up().wait_send()
 
 
-def fused_call(idx, piece, n_rows, n_cols):
-    n_tiles = idx.shape[1]
+def fused_call(tiles, piece, n_rows, n_cols):
+    n_tiles = tiles.shape[1] // n_cols
     slots = n_cols + 1
     chunk = piece.shape
     return pl.pallas_call(
         lambda *refs: fused_kernel(n_rows, n_cols, n_tiles, *refs),
-        out_shape=jax.ShapeDtypeStruct(chunk, jnp.float32),
+        out_shape=jax.ShapeDtypeStruct((chunk[0] * chunk[1] // 128, 128), jnp.float32),
         in_specs=[
             pl.BlockSpec(memory_space=pltpu.SMEM),
             pl.BlockSpec(memory_space=pltpu.VMEM),
@@ -310,22 +319,15 @@
             transcendentals=n_tiles * 2 * B,
         ),
         compiler_params=pltpu.CompilerParams(collective_id=0, has_side_effects=True),
-    )(idx, piece)
+    )(tiles, piece)
 
 
 def on_device(series, tile_list):
     piece = series.shape[0]
     col_count = lax.axis_size("cols")
     n_rows = lax.axis_size("rows")
-    group = lax.axis_index("rows")
-    col_id = lax.axis_index("cols")
-    per_dev = tile_list.shape[1] // col_count
-    mine = lax.dynamic_slice_in_dim(
-        tile_list[:2].reshape(2, per_dev, col_count), col_id, 1, axis=2
-    )[:, :, 0]
-    idx = jnp.stack([mine[0] - group * BPR, mine[1]])
-    result = fused_call(idx, series.reshape(SPILL, B), n_rows, col_count)
-    return result.reshape(piece)
+    result = fused_call(tile_list, series.reshape(SPILL, B), n_rows, col_count)
+    return jnp.maximum(result, jnp.float32(-1.0)).reshape(piece)
 
 
 def solution(mesh):

time: 49.4 us -> 48.7 us (0.986)
  local copies, waits for them, and re-layouts: 2.7 us -> 1.32 us
  other arithmetic: 0.81 us -> 1.33 us
    unnamed x3 -> x0, local copies, waits for them, and re-layouts: 1.33 us -> none
    reshape x0 -> x1, other arithmetic: none -> 1.33 us  [on_device(): return jnp.maximum(result, jnp.float32(-1.0)).reshape(piece)]
    slice x2 -> x0, local copies, waits for them, and re-layouts: 0.68 us -> none  [on_device(): tile_list[:2].reshape(2, per_dev, col_count)]
    reshape x2 -> x1, local copies, waits for them, and re-layouts: 0.69 us -> 1.32 us  [on_device(): result = fused_call(tile_list, series.reshape(SPILL, B), n_rows, col_count)]
    another operation x1 -> x0, other arithmetic: 0.59 us -> none  [on_device(): idx = jnp.stack([mine[0] - group * BPR, mine[1]])]
where the time goes in v6:
time: 48.7 us; the launch traced here: 48.3 us
  Pallas kernels  45.6 us (94%)
  other arithmetic  1.33 us (3%)
  local copies, waits for them, and re-layouts  1.32 us (3%)
    pallas_call x1, Pallas kernels, fused_call(): pl.pallas_call(lambda *refs: fused_kernel(n_rows, n_cols, n_tiles, *refs)...  45.6 us
    reshape x1, other arithmetic, on_device(): return jnp.maximum(result, jnp.float32(-1.0)).reshape(piece)  1.33 us
    reshape x1, local copies, waits for them, and re-layouts, on_device(): result = fused_call(tile_list, series.reshape(SPILL, B), n_rows, col_count)  1.32 us

profile of v6, /device:TPU:64, one launch (start us, length us, event | category | flops | bytes accessed | tf_op | source)
XLA Modules:
  0.0 48.3 jit_solution(16468443306187645708)
XLA Ops:
  0.0 1.3 %reshape.6.refs_1_ = f32[8,512]{1,0:T(8,128)} reshape(f32[4096]{0:T(1024)} %param.2) | data formatting | bytes 32768 | tf_op jit(solution)/shard_map/reshape | solution.py:329
  1.3 45.6 %shard_map.28 = f32[32,128]{1,0:T(8,128)} custom-call(s32[3,64]{1,0:T(4,128)} %refs_0_.1, f32[8,512]{1,0:T(8,128)} %reshape.6.refs_1_), custom_call_target="tpu_custom_call" | custom-call | flops 1610612736 | bytes 278528 | tf_op jit(solution)/shard_map/pallas_call | solution.py:297
  47.0 1.3 %maximum_bitcast_fusion = f32[4096]{0:T(1024)} fusion(f32[32,128]{1,0:T(8,128)} %shard_map.28), kind=kLoop, calls=%fused_computation | loop fusion | flops 4096 | bytes 32768 | tf_op jit(solution)/shard_map/reshape | solution.py:330

commit v7 on v6

--- a/solution.py
+++ b/solution.py
@@ -54,27 +54,27 @@
     c = lax.axis_index("cols")
     barrier = pltpu.get_barrier_semaphore()
     half = (c // 2) % 2
-    peers = [p for p in range(n_cols)]
-    for p in peers:
-        @pl.when(jnp.logical_and(p != c, jnp.logical_or((p // 2) % 2 == half, p == c ^ 2)))
+    for p in range(n_cols):
+        @pl.when(p != c)
         def _():
             pl.semaphore_signal(barrier, 1, device_id=(g, p), device_id_type=MESH)
 
+    has_next = g + 1 < n_rows
+
+    @pl.when(has_next)
+    def _():
+        pl.semaphore_signal(barrier, 1, device_id=(g + 1, 0), device_id_type=MESH)
+
+    down = jnp.logical_and(c == 0, g > 0)
+
+    @pl.when(down)
+    def _():
+        for p in range(n_cols):
+            pl.semaphore_signal(barrier, 1, device_id=(g - 1, p), device_id_type=MESH)
+
     collector = jnp.logical_or(c == 0, c == 2)
-    up = jnp.logical_and(collector, g + 1 < n_rows)
-
-    @pl.when(up)
-    def _():
-        pl.semaphore_signal(barrier, 1, device_id=(g + 1, 0), device_id_type=MESH)
-
-    down = jnp.logical_and(c == 0, g > 0)
-
-    @pl.when(down)
-    def _():
-        pl.semaphore_signal(barrier, 1, device_id=(g - 1, 0), device_id_type=MESH)
-        pl.semaphore_signal(barrier, 1, device_id=(g - 1, 2), device_id_type=MESH)
-
-    count = n_cols // 2 + up.astype(jnp.int32) + 2 * down.astype(jnp.int32)
+    up = jnp.logical_and(collector, has_next)
+    count = (n_cols - 1) + has_next.astype(jnp.int32) + n_cols * down.astype(jnp.int32)
     pl.semaphore_wait(barrier, count)
     return g, c, half, collector, up, down
 
@@ -86,10 +86,8 @@
 
 
 def fused_kernel(n_rows, n_cols, n_tiles, tiles_ref, piece_ref, out_ref,
-                 held, partial, got, mine, spills, g_send, g_recv, r_send, r_recv):
-    got[...] = jnp.full(got.shape, -1.0, jnp.float32)
+                 held, res, spill_out, spills, g_send, g_recv, r_send, r_recv, s_send, s_recv):
     spills[...] = jnp.full(spills.shape, -1.0, jnp.float32)
-    partial[...] = jnp.full(partial.shape, -1.0, jnp.float32)
     g, c, half, collector, up, down = greet_partners(n_rows, n_cols)
     mate = c ^ 2
     head = n_cols
@@ -150,6 +148,26 @@
     @pl.when(jnp.logical_and(jnp.logical_not(collector), g + 1 < n_rows))
     def _():
         remote(piece_ref, head, 1, (g, 0)).wait_recv()
+
+    def result_copy(p, sender, t):
+        return pltpu.make_async_remote_copy(
+            src_ref=res.at[sender, t],
+            dst_ref=res.at[sender, t],
+            send_sem=r_send.at[p],
+            recv_sem=r_recv.at[sender],
+            device_id=(g, p),
+            device_id_type=MESH,
+        )
+
+    def all_results(p, sender):
+        return pltpu.make_async_remote_copy(
+            src_ref=res.at[sender],
+            dst_ref=res.at[sender],
+            send_sem=r_send.at[p],
+            recv_sem=r_recv.at[sender],
+            device_id=(g, p),
+            device_id_type=MESH,
+        )
 
     r_i = lax.broadcasted_iota(jnp.int32, (B, B), 0)
     r_j = lax.broadcasted_iota(jnp.int32, (B, B), 1)
@@ -169,123 +187,107 @@
         col_r = jnp.max(corr, axis=0, keepdims=True)
         col_c = jnp.sum(jnp.where(flip, col_r, 0.0), axis=1, keepdims=True)
         col_max = jnp.sum(jnp.where(r_i == r_j, col_c, 0.0), axis=0, keepdims=True)
-        blk = lax.broadcasted_iota(jnp.int32, partial.shape, 0)
-        upd = jnp.maximum(
-            jnp.where(blk == i, row_max, jnp.float32(-1.0)),
-            jnp.where(blk == j, col_max, jnp.float32(-1.0)),
+        sub = lax.broadcasted_iota(jnp.int32, (8, 128), 0)
+        slab_v = jnp.full((8, 128), -1.0, jnp.float32)
+        for v in range(B // 128):
+            slab_v = jnp.where(sub == v, row_max[:, v * 128:(v + 1) * 128], slab_v)
+            slab_v = jnp.where(sub == 4 + v, col_max[:, v * 128:(v + 1) * 128], slab_v)
+        res[c, t] = slab_v
+        for p in range(n_cols):
+            @pl.when(p != c)
+            def _():
+                result_copy(p, c, t).start()
+        return carry
+
+    lax.fori_loop(0, n_tiles, body, 0)
+
+    has_next = g + 1 < n_rows
+    sub = lax.broadcasted_iota(jnp.int32, (8, 128), 0)
+    top = sub < 4
+
+    def gather_blocks(senders, base, acc):
+        for sender, t in senders:
+            col = sender + n_cols * t
+            i = jnp.clip(tiles_ref[0, col] - g * BPR, 0, BPR - 1) - base
+            j = i + jnp.clip(tiles_ref[1, col], 0, SPILL - 1)
+            slab_v = res[sender, t]
+            flipped = pltpu.roll(slab_v, 4, 0)
+            for m in range(len(acc)):
+                even, odd = 2 * m, 2 * m + 1
+                take = jnp.logical_or(jnp.logical_and(top, i == even), jnp.logical_and(jnp.logical_not(top), j == odd))
+                take_f = jnp.logical_or(jnp.logical_and(jnp.logical_not(top), i == odd), jnp.logical_and(top, j == even))
+                acc[m] = jnp.maximum(acc[m], jnp.maximum(
+                    jnp.where(take, slab_v, jnp.float32(-1.0)),
+                    jnp.where(take_f, flipped, jnp.float32(-1.0))))
+        return acc
+
+    quads = SPILL // 2
+    spill_acc = gather_blocks([(c, t) for t in range(n_tiles)], BPR,
+                              [jnp.full((8, 128), -1.0, jnp.float32) for _ in range(quads)])
+    for m in range(quads):
+        spill_out[pl.ds(8 * m, 8), :] = spill_acc[m]
+
+    def spill_up():
+        return pltpu.make_async_remote_copy(
+            src_ref=spill_out,
+            dst_ref=spills.at[c],
+            send_sem=s_send.at[0],
+            recv_sem=s_recv.at[0],
+            device_id=(g + 1, 0),
+            device_id_type=MESH,
         )
-        partial[...] = jnp.maximum(partial[...], upd)
-        return carry
-
-    lax.fori_loop(0, n_tiles, body, 0)
-
-    spill = n_cols
-
-    def rremote(src, dst, send, recv, device):
-        return pltpu.make_async_remote_copy(
-            src_ref=src,
-            dst_ref=dst,
-            send_sem=r_send.at[send],
-            recv_sem=r_recv.at[recv],
-            device_id=device,
-            device_id_type=MESH,
-        )
-
-    hub = 2 * half
-
-    def to_peer(p, k):
-        return rremote(slab(partial, p ^ (2 * k)), got.at[c, k], 3 * p + k, 2 * c + k, (g, p))
-
-    def from_peer(p, k):
-        return rremote(slab(partial, p), got.at[p, k], 3 * p + k, 2 * p + k, (g, p))
-
-    def spill_to_hub():
-        return rremote(slab(partial, spill), got.at[c, 2], 3 * n_cols, 2 * n_cols + 1 + c, (g, hub))
-
-    def spill_from(p):
-        return rremote(slab(partial, spill), got.at[p, 2], 3 * n_cols, 2 * n_cols + 1 + p, (g, p))
+
+    @pl.when(has_next)
+    def _():
+        spill_up().start()
+
+    for p in range(n_cols):
+        @pl.when(p != c)
+        def _():
+            all_results(p, p).wait_recv()
+
+    @pl.when(down)
+    def _():
+        pltpu.make_async_remote_copy(
+            src_ref=spills,
+            dst_ref=spills,
+            send_sem=s_send.at[0],
+            recv_sem=s_recv.at[0],
+            device_id=(g - 1, 0),
+            device_id_type=MESH,
+        ).wait_recv()
+
+    base = c * SPILL
+    acc = [jnp.full((8, 128), -1.0, jnp.float32) for _ in range(quads)]
+    for sender in range(n_cols):
+        acc = gather_blocks([(sender, t) for t in range(n_tiles)], base, acc)
+    spilled = jnp.max(spills[...], axis=0)
+    for m in range(quads):
+        out_ref[pl.ds(8 * m, 8), :] = jnp.maximum(acc[m], spilled[8 * m:8 * m + 8])
+
+    to_mate.wait_send()
+
+    @pl.when(down)
+    def _():
+        remote(piece_ref, head, 1, (g - 1, 0)).wait_send()
+        remote(piece_ref, head, 2, (g - 1, 2)).wait_send()
 
     for p, live in peers:
         @pl.when(live)
         def _():
-            to_peer(p, 0).start()
-            to_peer(p, 1).start()
-
-    @pl.when(jnp.logical_not(collector))
-    def _():
-        spill_to_hub().start()
-
-    for p, live in peers:
-        @pl.when(live)
-        def _():
-            from_peer(p, 0).wait_recv()
-            from_peer(p, 1).wait_recv()
-
-    own = partial[pl.ds(pl.multiple_of(c * rows, rows), rows), :]
-    mate_part = partial[pl.ds(pl.multiple_of(mate * rows, rows), rows), :]
-    acc = jnp.maximum(own, jnp.max(got[:, 0], axis=0))
-    mine[0] = jnp.maximum(mate_part, jnp.max(got[:, 1], axis=0))
-
-    to_mate_r = rremote(mine.at[0], mine.at[1], 3 * n_cols + 1, 3 * n_cols + 1, (g, mate))
-    to_mate_r.start()
-
-    @pl.when(collector)
-    def _():
-        for p, live in peers:
-            @pl.when(live)
-            def _():
-                spill_from(p).wait_recv()
-
-    mine[2] = jnp.maximum(partial[pl.ds(spill * rows, rows), :], jnp.max(got[:, 2], axis=0))
-
-    def spill_up():
-        return rremote(mine.at[2], spills.at[half], 3 * n_cols + 2, 3 * n_cols + 2 + half, (g + 1, 0))
-
-    @pl.when(up)
-    def _():
-        spill_up().start()
-
-    to_mate_r.wait_recv()
-
-    @pl.when(down)
-    def _():
-        rremote(mine.at[2], spills.at[0], 3 * n_cols + 2, 3 * n_cols + 2, (g - 1, 0)).wait_recv()
-        rremote(mine.at[2], spills.at[1], 3 * n_cols + 2, 3 * n_cols + 3, (g - 1, 2)).wait_recv()
-
-    acc = jnp.maximum(acc, mine[1])
-    acc = jnp.maximum(acc, jnp.maximum(spills[0], spills[1]))
-    lanes = 128
-    per_row = B // lanes
-    for k in range(rows):
-        for v in range(per_row):
-            out_ref[pl.ds(k * per_row + v, 1), :] = acc[k:k + 1, v * lanes:(v + 1) * lanes]
-
-    to_mate.wait_send()
-
-    @pl.when(down)
-    def _():
-        remote(piece_ref, head, 1, (g - 1, 0)).wait_send()
-        remote(piece_ref, head, 2, (g - 1, 2)).wait_send()
-
-    for p, live in peers:
-        @pl.when(live)
-        def _():
             remote(piece_ref, c, 3 + 3 * p, (g, p)).wait_send()
             remote(piece_ref, c, 4 + 3 * p, (g, p)).wait_send()
-            to_peer(p, 0).wait_send()
-            to_peer(p, 1).wait_send()
 
         @pl.when(jnp.logical_and(live, up))
         def _():
             remote(piece_ref, c, 5 + 3 * p, (g, p)).wait_send()
 
-    @pl.when(jnp.logical_not(collector))
-    def _():
-        spill_to_hub().wait_send()
-
-    to_mate_r.wait_send()
-
-    @pl.when(up)
+    for p in range(n_cols):
+        @pl.when(p != c)
+        def _():
+            all_results(p, c).wait_send()
+
+    @pl.when(has_next)
     def _():
         spill_up().wait_send()
 
@@ -304,14 +306,15 @@
         out_specs=pl.BlockSpec(memory_space=pltpu.VMEM),
         scratch_shapes=[
             pltpu.VMEM((slots * chunk[0], B), jnp.float32),
-            pltpu.VMEM((slots * chunk[0], B), jnp.float32),
-            pltpu.VMEM((n_cols, 3) + chunk, jnp.float32),
-            pltpu.VMEM((3,) + chunk, jnp.float32),
-            pltpu.VMEM((2,) + chunk, jnp.float32),
+            pltpu.VMEM((n_cols, n_tiles, 8, 128), jnp.float32),
+            pltpu.VMEM((chunk[0] * chunk[1] // 128, 128), jnp.float32),
+            pltpu.VMEM((n_cols, chunk[0] * chunk[1] // 128, 128), jnp.float32),
             pltpu.SemaphoreType.DMA((3 + 3 * n_cols,)),
             pltpu.SemaphoreType.DMA((slots,)),
-            pltpu.SemaphoreType.DMA((3 * n_cols + 3,)),
-            pltpu.SemaphoreType.DMA((3 * n_cols + 4,)),
+            pltpu.SemaphoreType.DMA((n_cols,)),
+            pltpu.SemaphoreType.DMA((n_cols,)),
+            pltpu.SemaphoreType.DMA((1,)),
+            pltpu.SemaphoreType.DMA((1,)),
         ],
         cost_estimate=pl.CostEstimate(
             flops=n_tiles * 2 * B * B * M * 3,

time: 48.7 us -> 47.8 us (0.982)
  Pallas kernels: 45.6 us -> 44.7 us
    pallas_call x1, Pallas kernels: 45.6 us -> 44.7 us  [fused_call(): pl.pallas_call(lambda *refs: fused_kernel(n_rows, n_cols, n_tiles, *refs)...]
where the time goes in v7:
time: 47.8 us; the launch traced here: 47.4 us
  Pallas kernels  44.7 us (94%)
  other arithmetic  1.33 us (3%)
  local copies, waits for them, and re-layouts  1.32 us (3%)
    pallas_call x1, Pallas kernels, fused_call(): pl.pallas_call(lambda *refs: fused_kernel(n_rows, n_cols, n_tiles, *refs)...  44.7 us
    reshape x1, other arithmetic, on_device(): return jnp.maximum(result, jnp.float32(-1.0)).reshape(piece)  1.33 us
    reshape x1, local copies, waits for them, and re-layouts, on_device(): result = fused_call(tile_list, series.reshape(SPILL, B), n_rows, col_count)  1.32 us

profile of v7, /device:TPU:64, one launch (start us, length us, event | category | flops | bytes accessed | tf_op | source)
XLA Modules:
  0.0 47.4 jit_solution(2883410464094227469)
XLA Ops:
  0.0 1.3 %reshape.6.refs_1_ = f32[8,512]{1,0:T(8,128)} reshape(f32[4096]{0:T(1024)} %param.2) | data formatting | bytes 32768 | tf_op jit(solution)/shard_map/reshape | solution.py:332
  1.3 44.7 %shard_map.28 = f32[32,128]{1,0:T(8,128)} custom-call(s32[3,64]{1,0:T(4,128)} %refs_0_.1, f32[8,512]{1,0:T(8,128)} %reshape.6.refs_1_), custom_call_target="tpu_custom_call" | custom-call | flops 1610612736 | bytes 278528 | tf_op jit(solution)/shard_map/pallas_call | solution.py:299
  46.1 1.3 %maximum_bitcast_fusion = f32[4096]{0:T(1024)} fusion(f32[32,128]{1,0:T(8,128)} %shard_map.28), kind=kLoop, calls=%fused_computation | loop fusion | flops 4096 | bytes 32768 | tf_op jit(solution)/shard_map/reshape | solution.py:333

commit v8 on v7

--- a/solution.py
+++ b/solution.py
@@ -23,7 +23,8 @@
 
 
 def windows(held, b):
-    seg = jnp.concatenate([held[pl.ds(b, 1), :], held[pl.ds(b + 1, 1), :][:, :M]], axis=1)
+    per = B // 128
+    seg = jnp.concatenate([held[pl.ds(b * per + v, 1), :] for v in range(SEG // 128)], axis=1)
     parts = []
     for m in range(B // 128):
         lo = 3 * 128 - 128 * m
@@ -91,7 +92,7 @@
     g, c, half, collector, up, down = greet_partners(n_rows, n_cols)
     mate = c ^ 2
     head = n_cols
-    rows = SPILL
+    rows = SPILL * B // 128
     peers = half_peers(n_cols, c, half)
 
     def slab(ref, k):
@@ -298,17 +299,17 @@
     chunk = piece.shape
     return pl.pallas_call(
         lambda *refs: fused_kernel(n_rows, n_cols, n_tiles, *refs),
-        out_shape=jax.ShapeDtypeStruct((chunk[0] * chunk[1] // 128, 128), jnp.float32),
+        out_shape=jax.ShapeDtypeStruct(chunk, jnp.float32),
         in_specs=[
             pl.BlockSpec(memory_space=pltpu.SMEM),
             pl.BlockSpec(memory_space=pltpu.VMEM),
         ],
         out_specs=pl.BlockSpec(memory_space=pltpu.VMEM),
         scratch_shapes=[
-            pltpu.VMEM((slots * chunk[0], B), jnp.float32),
+            pltpu.VMEM((slots * chunk[0], 128), jnp.float32),
             pltpu.VMEM((n_cols, n_tiles, 8, 128), jnp.float32),
-            pltpu.VMEM((chunk[0] * chunk[1] // 128, 128), jnp.float32),
-            pltpu.VMEM((n_cols, chunk[0] * chunk[1] // 128, 128), jnp.float32),
+            pltpu.VMEM(chunk, jnp.float32),
+            pltpu.VMEM((n_cols,) + chunk, jnp.float32),
             pltpu.SemaphoreType.DMA((3 + 3 * n_cols,)),
             pltpu.SemaphoreType.DMA((slots,)),
             pltpu.SemaphoreType.DMA((n_cols,)),
@@ -318,7 +319,7 @@
         ],
         cost_estimate=pl.CostEstimate(
             flops=n_tiles * 2 * B * B * M * 3,
-            bytes_accessed=slots * chunk[0] * B * 4,
+            bytes_accessed=slots * chunk[0] * 128 * 4,
             transcendentals=n_tiles * 2 * B,
         ),
         compiler_params=pltpu.CompilerParams(collective_id=0, has_side_effects=True),
@@ -329,7 +330,7 @@
     piece = series.shape[0]
     col_count = lax.axis_size("cols")
     n_rows = lax.axis_size("rows")
-    result = fused_call(tile_list, series.reshape(SPILL, B), n_rows, col_count)
+    result = fused_call(tile_list, series.reshape(piece // 128, 128), n_rows, col_count)
     return jnp.maximum(result, jnp.float32(-1.0)).reshape(piece)
 
 

time: 47.8 us -> 46.4 us (0.971)
  local copies, waits for them, and re-layouts: 1.32 us -> 0 us
    reshape x1 -> x0, local copies, waits for them, and re-layouts: 1.32 us -> none  [on_device(): result = fused_call(tile_list, series.reshape(SPILL, B), n_rows, col_count)]
where the time goes in v8:
time: 46.4 us; the launch traced here: 46.1 us
  Pallas kernels  44.7 us (96%)
  other arithmetic  1.33 us (3%)
    pallas_call x1, Pallas kernels, fused_call(): pl.pallas_call(lambda *refs: fused_kernel(n_rows, n_cols, n_tiles, *refs)...  44.7 us
    reshape x1, other arithmetic, on_device(): return jnp.maximum(result, jnp.float32(-1.0)).reshape(piece)  1.33 us

profile of v8, /device:TPU:64, one launch (start us, length us, event | category | flops | bytes accessed | tf_op | source)
XLA Modules:
  0.0 46.1 jit_solution(6152960210220177938)
XLA Ops:
  0.0 44.7 %shard_map.28 = f32[32,128]{1,0:T(8,128)} custom-call(s32[3,64]{1,0:T(4,128)} %refs_0_.1, f32[32,128]{1,0:T(8,128)} %bitcast.3), custom_call_target="tpu_custom_call" | custom-call | flops 1610612736 | bytes 278528 | tf_op jit(solution)/shard_map/pallas_call | solution.py:300
  44.7 1.3 %maximum_bitcast_fusion = f32[4096]{0:T(1024)} fusion(f32[32,128]{1,0:T(8,128)} %shard_map.28), kind=kLoop, calls=%fused_computation | loop fusion | flops 4096 | bytes 32768 | tf_op jit(solution)/shard_map/reshape | solution.py:334

commit v9 on v8

--- a/solution.py
+++ b/solution.py
@@ -242,10 +242,15 @@
     def _():
         spill_up().start()
 
-    for p in range(n_cols):
-        @pl.when(p != c)
-        def _():
-            all_results(p, p).wait_recv()
+
+    base = c * SPILL
+    acc = [jnp.full((8, 128), -1.0, jnp.float32) for _ in range(quads)]
+    for sender in range(n_cols):
+        @pl.when(sender != c)
+        def _():
+            all_results(sender, sender).wait_recv()
+
+        acc = gather_blocks([(sender, t) for t in range(n_tiles)], base, acc)
 
     @pl.when(down)
     def _():
@@ -258,10 +263,6 @@
             device_id_type=MESH,
         ).wait_recv()
 
-    base = c * SPILL
-    acc = [jnp.full((8, 128), -1.0, jnp.float32) for _ in range(quads)]
-    for sender in range(n_cols):
-        acc = gather_blocks([(sender, t) for t in range(n_tiles)], base, acc)
     spilled = jnp.max(spills[...], axis=0)
     for m in range(quads):
         out_ref[pl.ds(8 * m, 8), :] = jnp.maximum(acc[m], spilled[8 * m:8 * m + 8])

time: 46.4 us -> 45.1 us (0.972)
  the two profiles are of different devices: /device:TPU:64 before, /device:TPU:25 now
where the time goes in v9:
time: 45.1 us; the launch traced here: 44.8 us
  Pallas kernels  43.5 us (96%)
  other arithmetic  1.33 us (3%)
    pallas_call x1, Pallas kernels, fused_call(): pl.pallas_call(lambda *refs: fused_kernel(n_rows, n_cols, n_tiles, *refs)...  43.5 us
    reshape x1, other arithmetic, on_device(): return jnp.maximum(result, jnp.float32(-1.0)).reshape(piece)  1.33 us

profile of v9, /device:TPU:25, one launch (start us, length us, event | category | flops | bytes accessed | tf_op | source)
XLA Modules:
  0.0 44.8 jit_solution(15934392414624167527)
XLA Ops:
  0.0 43.5 %shard_map.28 = f32[32,128]{1,0:T(8,128)} custom-call(s32[3,64]{1,0:T(4,128)} %refs_0_.1, f32[32,128]{1,0:T(8,128)} %bitcast.3), custom_call_target="tpu_custom_call" | custom-call | flops 1610612736 | bytes 278528 | tf_op jit(solution)/shard_map/pallas_call | solution.py:301
  43.5 1.3 %maximum_bitcast_fusion = f32[4096]{0:T(1024)} fusion(f32[32,128]{1,0:T(8,128)} %shard_map.28), kind=kLoop, calls=%fused_computation | loop fusion | flops 4096 | bytes 32768 | tf_op jit(solution)/shard_map/reshape | solution.py:335

commit v10 on v9

--- a/solution.py
+++ b/solution.py
@@ -50,6 +50,18 @@
     return dot(a_hi, b_hi) + (dot(a_hi, b_lo) + dot(a_lo, b_hi))
 
 
+def reverse_lanes(x, mirror):
+    hi = x.astype(jnp.bfloat16)
+    rest = x - hi.astype(jnp.float32)
+    mid = rest.astype(jnp.bfloat16)
+    lo = (rest - mid.astype(jnp.float32)).astype(jnp.bfloat16)
+
+    def dot(part):
+        return jnp.dot(part, mirror, preferred_element_type=jnp.float32)
+
+    return (dot(hi) + dot(mid)) + dot(lo)
+
+
 def greet_partners(n_rows, n_cols):
     g = lax.axis_index("rows")
     c = lax.axis_index("cols")
@@ -173,6 +185,9 @@
     r_i = lax.broadcasted_iota(jnp.int32, (B, B), 0)
     r_j = lax.broadcasted_iota(jnp.int32, (B, B), 1)
     flip = r_i + r_j == B - 1
+    m_i = lax.broadcasted_iota(jnp.int32, (128, 128), 0)
+    m_j = lax.broadcasted_iota(jnp.int32, (128, 128), 1)
+    mirror = jnp.where(m_i + m_j == 127, 1.0, 0.0).astype(jnp.bfloat16)
 
     def body(t, carry):
         col = c + n_cols * t
@@ -186,13 +201,13 @@
         row_c = jnp.max(corr, axis=1, keepdims=True)
         row_max = jnp.sum(jnp.where(flip, row_c, 0.0), axis=0, keepdims=True)
         col_r = jnp.max(corr, axis=0, keepdims=True)
-        col_c = jnp.sum(jnp.where(flip, col_r, 0.0), axis=1, keepdims=True)
-        col_max = jnp.sum(jnp.where(r_i == r_j, col_c, 0.0), axis=0, keepdims=True)
         sub = lax.broadcasted_iota(jnp.int32, (8, 128), 0)
         slab_v = jnp.full((8, 128), -1.0, jnp.float32)
-        for v in range(B // 128):
+        nb = B // 128
+        for v in range(nb):
             slab_v = jnp.where(sub == v, row_max[:, v * 128:(v + 1) * 128], slab_v)
-            slab_v = jnp.where(sub == 4 + v, col_max[:, v * 128:(v + 1) * 128], slab_v)
+            slab_v = jnp.where(sub == nb + v, col_r[:, (nb - 1 - v) * 128:(nb - v) * 128], slab_v)
+        slab_v = jnp.where(sub < nb, slab_v, reverse_lanes(slab_v, mirror))
         res[c, t] = slab_v
         for p in range(n_cols):
             @pl.when(p != c)

time: 45.1 us -> 44.6 us (0.989)
  the two profiles are of different devices: /device:TPU:25 before, /device:TPU:64 now
where the time goes in v10:
time: 44.6 us; the launch traced here: 44.3 us
  Pallas kernels  43 us (96%)
  other arithmetic  1.33 us (3%)
    pallas_call x1, Pallas kernels, fused_call(): pl.pallas_call(lambda *refs: fused_kernel(n_rows, n_cols, n_tiles, *refs)...  43 us
    reshape x1, other arithmetic, on_device(): return jnp.maximum(result, jnp.float32(-1.0)).reshape(piece)  1.33 us

profile of v10, /device:TPU:64, one launch (start us, length us, event | category | flops | bytes accessed | tf_op | source)
XLA Modules:
  0.0 44.3 jit_solution(18364653169501260218)
XLA Ops:
  0.0 43.0 %shard_map.28 = f32[32,128]{1,0:T(8,128)} custom-call(s32[3,64]{1,0:T(4,128)} %refs_0_.1, f32[32,128]{1,0:T(8,128)} %bitcast.3), custom_call_target="tpu_custom_call" | custom-call | flops 1610612736 | bytes 278528 | tf_op jit(solution)/shard_map/pallas_call | solution.py:316
  43.0 1.3 %maximum_bitcast_fusion = f32[4096]{0:T(1024)} fusion(f32[32,128]{1,0:T(8,128)} %shard_map.28), kind=kLoop, calls=%fused_computation | loop fusion | flops 4096 | bytes 32768 | tf_op jit(solution)/shard_map/reshape | solution.py:350

commit v11 on v10

--- a/solution.py
+++ b/solution.py
@@ -99,8 +99,13 @@
 
 
 def fused_kernel(n_rows, n_cols, n_tiles, tiles_ref, piece_ref, out_ref,
-                 held, res, spill_out, spills, g_send, g_recv, r_send, r_recv, s_send, s_recv):
+                 held, res, spill_out, spills, diff_ref, flip_ref,
+                 g_send, g_recv, r_send, r_recv, s_send, s_recv):
     spills[...] = jnp.full(spills.shape, -1.0, jnp.float32)
+    r_i = lax.broadcasted_iota(jnp.int32, (B, B), 0)
+    r_j = lax.broadcasted_iota(jnp.int32, (B, B), 1)
+    diff_ref[...] = r_i - r_j
+    flip_ref[...] = jnp.where(r_i + r_j == B - 1, 1.0, 0.0)
     g, c, half, collector, up, down = greet_partners(n_rows, n_cols)
     mate = c ^ 2
     head = n_cols
@@ -182,9 +187,6 @@
             device_id_type=MESH,
         )
 
-    r_i = lax.broadcasted_iota(jnp.int32, (B, B), 0)
-    r_j = lax.broadcasted_iota(jnp.int32, (B, B), 1)
-    flip = r_i + r_j == B - 1
     m_i = lax.broadcasted_iota(jnp.int32, (128, 128), 0)
     m_j = lax.broadcasted_iota(jnp.int32, (128, 128), 1)
     mirror = jnp.where(m_i + m_j == 127, 1.0, 0.0).astype(jnp.bfloat16)
@@ -197,9 +199,9 @@
         zl = windows(held, i)
         zr = windows(held, j)
         corr = split_dot(zl, zr)
-        corr = jnp.where(d * B + r_i - r_j >= EXCL, corr, jnp.float32(-1.0))
+        corr = jnp.where(diff_ref[...] >= EXCL - d * B, corr, jnp.float32(-1.0))
         row_c = jnp.max(corr, axis=1, keepdims=True)
-        row_max = jnp.sum(jnp.where(flip, row_c, 0.0), axis=0, keepdims=True)
+        row_max = jnp.sum(row_c * flip_ref[...], axis=0, keepdims=True)
         col_r = jnp.max(corr, axis=0, keepdims=True)
         sub = lax.broadcasted_iota(jnp.int32, (8, 128), 0)
         slab_v = jnp.full((8, 128), -1.0, jnp.float32)
@@ -326,6 +328,8 @@
             pltpu.VMEM((n_cols, n_tiles, 8, 128), jnp.float32),
             pltpu.VMEM(chunk, jnp.float32),
             pltpu.VMEM((n_cols,) + chunk, jnp.float32),
+            pltpu.VMEM((B, B), jnp.int32),
+            pltpu.VMEM((B, B), jnp.float32),
             pltpu.SemaphoreType.DMA((3 + 3 * n_cols,)),
             pltpu.SemaphoreType.DMA((slots,)),
             pltpu.SemaphoreType.DMA((n_cols,)),

time: 44.6 us -> 44.8 us (level)
  the two profiles are of different devices: /device:TPU:64 before, /device:TPU:25 now
where the time goes in v11:
time: 44.8 us; the launch traced here: 44.5 us
  Pallas kernels  43.2 us (96%)
  other arithmetic  1.33 us (3%)
    pallas_call x1, Pallas kernels, fused_call(): pl.pallas_call(lambda *refs: fused_kernel(n_rows, n_cols, n_tiles, *refs)...  43.2 us
    reshape x1, other arithmetic, on_device(): return jnp.maximum(result, jnp.float32(-1.0)).reshape(piece)  1.33 us

profile of v11, /device:TPU:25, one launch (start us, length us, event | category | flops | bytes accessed | tf_op | source)
XLA Modules:
  0.0 44.5 jit_solution(17225975184565830252)
XLA Ops:
  0.0 43.2 %shard_map.28 = f32[32,128]{1,0:T(8,128)} custom-call(s32[3,64]{1,0:T(4,128)} %refs_0_.1, f32[32,128]{1,0:T(8,128)} %bitcast.3), custom_call_target="tpu_custom_call" | custom-call | flops 1610612736 | bytes 278528 | tf_op jit(solution)/shard_map/pallas_call | solution.py:318
  43.2 1.3 %maximum_bitcast_fusion = f32[4096]{0:T(1024)} fusion(f32[32,128]{1,0:T(8,128)} %shard_map.28), kind=kLoop, calls=%fused_computation | loop fusion | flops 4096 | bytes 32768 | tf_op jit(solution)/shard_map/reshape | solution.py:354

commit v12 on v11

--- a/solution.py
+++ b/solution.py
@@ -130,6 +130,11 @@
     to_mate = remote(piece_ref, c, 0, (g, mate))
     to_mate.start()
 
+    for p, live in peers:
+        @pl.when(live)
+        def _():
+            remote(piece_ref, c, 3 + 3 * p, (g, p)).start()
+
     @pl.when(down)
     def _():
         remote(piece_ref, head, 1, (g - 1, 0)).start()
@@ -148,7 +153,6 @@
     for p, live in peers:
         @pl.when(live)
         def _():
-            remote(piece_ref, c, 3 + 3 * p, (g, p)).start()
             remote(slab(held, mate), mate, 4 + 3 * p, (g, p)).start()
 
         @pl.when(jnp.logical_and(live, up))
@@ -217,7 +221,7 @@
                 result_copy(p, c, t).start()
         return carry
 
-    lax.fori_loop(0, n_tiles, body, 0)
+    lax.fori_loop(0, n_tiles, body, 0, unroll=True)
 
     has_next = g + 1 < n_rows
     sub = lax.broadcasted_iota(jnp.int32, (8, 128), 0)

time: 44.8 us -> 44.3 us (0.989)
  Pallas kernels: 43.2 us -> 42.7 us
    pallas_call x1, Pallas kernels: 43.2 us -> 42.7 us  [fused_call(): pl.pallas_call(lambda *refs: fused_kernel(n_rows, n_cols, n_tiles, *refs)...]
where the time goes in v12:
time: 44.3 us; the launch traced here: 44 us
  Pallas kernels  42.7 us (96%)
  other arithmetic  1.33 us (3%)
    pallas_call x1, Pallas kernels, fused_call(): pl.pallas_call(lambda *refs: fused_kernel(n_rows, n_cols, n_tiles, *refs)...  42.7 us
    reshape x1, other arithmetic, on_device(): return jnp.maximum(result, jnp.float32(-1.0)).reshape(piece)  1.33 us

profile of v12, /device:TPU:25, one launch (start us, length us, event | category | flops | bytes accessed | tf_op | source)
XLA Modules:
  0.0 44.0 jit_solution(5290648287084070181)
XLA Ops:
  0.0 42.7 %shard_map.28 = f32[32,128]{1,0:T(8,128)} custom-call(s32[3,64]{1,0:T(4,128)} %refs_0_.1, f32[32,128]{1,0:T(8,128)} %bitcast.3), custom_call_target="tpu_custom_call" | custom-call | flops 1610612736 | bytes 278528 | tf_op jit(solution)/shard_map/pallas_call | solution.py:322
  42.7 1.3 %maximum_bitcast_fusion = f32[4096]{0:T(1024)} fusion(f32[32,128]{1,0:T(8,128)} %shard_map.28), kind=kLoop, calls=%fused_computation | loop fusion | flops 4096 | bytes 32768 | tf_op jit(solution)/shard_map/reshape | solution.py:358

commit v13 on v12

--- a/solution.py
+++ b/solution.py
@@ -62,7 +62,7 @@
     return (dot(hi) + dot(mid)) + dot(lo)
 
 
-def greet_partners(n_rows, n_cols):
+def greet_partners(n_rows, n_cols, before_wait):
     g = lax.axis_index("rows")
     c = lax.axis_index("cols")
     barrier = pltpu.get_barrier_semaphore()
@@ -88,6 +88,7 @@
     collector = jnp.logical_or(c == 0, c == 2)
     up = jnp.logical_and(collector, has_next)
     count = (n_cols - 1) + has_next.astype(jnp.int32) + n_cols * down.astype(jnp.int32)
+    before_wait()
     pl.semaphore_wait(barrier, count)
     return g, c, half, collector, up, down
 
@@ -102,11 +103,14 @@
                  held, res, spill_out, spills, diff_ref, flip_ref,
                  g_send, g_recv, r_send, r_recv, s_send, s_recv):
     spills[...] = jnp.full(spills.shape, -1.0, jnp.float32)
-    r_i = lax.broadcasted_iota(jnp.int32, (B, B), 0)
-    r_j = lax.broadcasted_iota(jnp.int32, (B, B), 1)
-    diff_ref[...] = r_i - r_j
-    flip_ref[...] = jnp.where(r_i + r_j == B - 1, 1.0, 0.0)
-    g, c, half, collector, up, down = greet_partners(n_rows, n_cols)
+
+    def tables():
+        r_i = lax.broadcasted_iota(jnp.int32, (B, B), 0)
+        r_j = lax.broadcasted_iota(jnp.int32, (B, B), 1)
+        diff_ref[...] = r_i - r_j
+        flip_ref[...] = jnp.where(r_i + r_j == B - 1, 1.0, 0.0)
+
+    g, c, half, collector, up, down = greet_partners(n_rows, n_cols, tables)
     mate = c ^ 2
     head = n_cols
     rows = SPILL * B // 128

time: 44.3 us -> 44.2 us (level)
  no operation moved by 1% of the time
where the time goes in v13:
time: 44.2 us; the launch traced here: 43.9 us
  Pallas kernels  42.5 us (96%)
  other arithmetic  1.33 us (3%)
    pallas_call x1, Pallas kernels, fused_call(): pl.pallas_call(lambda *refs: fused_kernel(n_rows, n_cols, n_tiles, *refs)...  42.5 us
    reshape x1, other arithmetic, on_device(): return jnp.maximum(result, jnp.float32(-1.0)).reshape(piece)  1.33 us

profile of v13, /device:TPU:25, one launch (start us, length us, event | category | flops | bytes accessed | tf_op | source)
XLA Modules:
  0.0 43.9 jit_solution(10343953003696123647)
XLA Ops:
  0.0 42.5 %shard_map.28 = f32[32,128]{1,0:T(8,128)} custom-call(s32[3,64]{1,0:T(4,128)} %refs_0_.1, f32[32,128]{1,0:T(8,128)} %bitcast.3), custom_call_target="tpu_custom_call" | custom-call | flops 1610612736 | bytes 278528 | tf_op jit(solution)/shard_map/pallas_call | solution.py:326
  42.5 1.3 %maximum_bitcast_fusion = f32[4096]{0:T(1024)} fusion(f32[32,128]{1,0:T(8,128)} %shard_map.28), kind=kLoop, calls=%fused_computation | loop fusion | flops 4096 | bytes 32768 | tf_op jit(solution)/shard_map/reshape | solution.py:362

commit v14 on v13

--- a/solution.py
+++ b/solution.py
@@ -47,7 +47,9 @@
     def dot(x, y):
         return lax.dot_general(x, y, dims, preferred_element_type=jnp.float32)
 
-    return dot(a_hi, b_hi) + (dot(a_hi, b_lo) + dot(a_lo, b_hi))
+    lhs = jnp.concatenate([a_hi, a_hi, a_lo], axis=1)
+    rhs = jnp.concatenate([b_hi, b_lo, b_hi], axis=1)
+    return dot(lhs, rhs)
 
 
 def reverse_lanes(x, mirror):

time: 44.2 us -> 44.2 us (level)
  no operation moved by 1% of the time
where the time goes in v14:
time: 44.2 us; the launch traced here: 43.9 us
  Pallas kernels  42.5 us (96%)
  other arithmetic  1.33 us (3%)
    pallas_call x1, Pallas kernels, fused_call(): pl.pallas_call(lambda *refs: fused_kernel(n_rows, n_cols, n_tiles, *refs)...  42.5 us
    reshape x1, other arithmetic, on_device(): return jnp.maximum(result, jnp.float32(-1.0)).reshape(piece)  1.33 us

profile of v14, /device:TPU:25, one launch (start us, length us, event | category | flops | bytes accessed | tf_op | source)
XLA Modules:
  0.0 43.9 jit_solution(3545098935382416645)
XLA Ops:
  0.0 42.5 %shard_map.28 = f32[32,128]{1,0:T(8,128)} custom-call(s32[3,64]{1,0:T(4,128)} %refs_0_.1, f32[32,128]{1,0:T(8,128)} %bitcast.3), custom_call_target="tpu_custom_call" | custom-call | flops 1610612736 | bytes 278528 | tf_op jit(solution)/shard_map/pallas_call | solution.py:328
  42.5 1.3 %maximum_bitcast_fusion = f32[4096]{0:T(1024)} fusion(f32[32,128]{1,0:T(8,128)} %shard_map.28), kind=kLoop, calls=%fused_computation | loop fusion | flops 4096 | bytes 32768 | tf_op jit(solution)/shard_map/reshape | solution.py:364

commit v15 on v13

--- a/solution.py
+++ b/solution.py
@@ -150,15 +150,16 @@
 
     remote(piece_ref, mate, 0, (g, mate)).wait_recv()
 
+    for p, live in peers:
+        @pl.when(live)
+        def _():
+            remote(slab(held, mate), mate, 4 + 3 * p, (g, p)).start()
+
     @pl.when(up)
     def _():
         remote(piece_ref, head, 1, (g + 1, 0)).wait_recv()
 
     for p, live in peers:
-        @pl.when(live)
-        def _():
-            remote(slab(held, mate), mate, 4 + 3 * p, (g, p)).start()
-
         @pl.when(jnp.logical_and(live, up))
         def _():
             remote(slab(held, head), head, 5 + 3 * p, (g, p)).start()

time: 44.2 us -> 43.6 us (0.986)
  Pallas kernels: 42.5 us -> 41.9 us
    pallas_call x1, Pallas kernels: 42.5 us -> 41.9 us  [fused_call(): pl.pallas_call(lambda *refs: fused_kernel(n_rows, n_cols, n_tiles, *refs)...]
where the time goes in v15:
time: 43.6 us; the launch traced here: 43.2 us
  Pallas kernels  41.9 us (96%)
  other arithmetic  1.33 us (3%)
    pallas_call x1, Pallas kernels, fused_call(): pl.pallas_call(lambda *refs: fused_kernel(n_rows, n_cols, n_tiles, *refs)...  41.9 us
    reshape x1, other arithmetic, on_device(): return jnp.maximum(result, jnp.float32(-1.0)).reshape(piece)  1.33 us

profile of v15, /device:TPU:25, one launch (start us, length us, event | category | flops | bytes accessed | tf_op | source)
XLA Modules:
  0.0 43.2 jit_solution(781409400839084351)
XLA Ops:
  0.0 41.9 %shard_map.28 = f32[32,128]{1,0:T(8,128)} custom-call(s32[3,64]{1,0:T(4,128)} %refs_0_.1, f32[32,128]{1,0:T(8,128)} %bitcast.3), custom_call_target="tpu_custom_call" | custom-call | flops 1610612736 | bytes 278528 | tf_op jit(solution)/shard_map/pallas_call | solution.py:327
  41.9 1.3 %maximum_bitcast_fusion = f32[4096]{0:T(1024)} fusion(f32[32,128]{1,0:T(8,128)} %shard_map.28), kind=kLoop, calls=%fused_computation | loop fusion | flops 4096 | bytes 32768 | tf_op jit(solution)/shard_map/reshape | solution.py:363

commit v16 on v15

--- a/solution.py
+++ b/solution.py
@@ -220,10 +220,12 @@
             slab_v = jnp.where(sub == nb + v, col_r[:, (nb - 1 - v) * 128:(nb - v) * 128], slab_v)
         slab_v = jnp.where(sub < nb, slab_v, reverse_lanes(slab_v, mirror))
         res[c, t] = slab_v
-        for p in range(n_cols):
-            @pl.when(p != c)
-            def _():
-                result_copy(p, c, t).start()
+        for near in (False, True):
+            for p in range(n_cols):
+                same = ((p // 2) % 2 == half)
+                @pl.when(jnp.logical_and(p != c, same == near))
+                def _():
+                    result_copy(p, c, t).start()
         return carry
 
     lax.fori_loop(0, n_tiles, body, 0, unroll=True)

time: 43.6 us -> 43.3 us (level)
  no operation moved by 1% of the time
where the time goes in v16:
time: 43.3 us; the launch traced here: 43 us
  Pallas kernels  41.7 us (96%)
  other arithmetic  1.33 us (3%)
    pallas_call x1, Pallas kernels, fused_call(): pl.pallas_call(lambda *refs: fused_kernel(n_rows, n_cols, n_tiles, *refs)...  41.7 us
    reshape x1, other arithmetic, on_device(): return jnp.maximum(result, jnp.float32(-1.0)).reshape(piece)  1.33 us

profile of v16, /device:TPU:25, one launch (start us, length us, event | category | flops | bytes accessed | tf_op | source)
XLA Modules:
  0.0 43.0 jit_solution(2517937300953350932)
XLA Ops:
  0.0 41.7 %shard_map.28 = f32[32,128]{1,0:T(8,128)} custom-call(s32[3,64]{1,0:T(4,128)} %refs_0_.1, f32[32,128]{1,0:T(8,128)} %bitcast.3), custom_call_target="tpu_custom_call" | custom-call | flops 1610612736 | bytes 278528 | tf_op jit(solution)/shard_map/pallas_call | solution.py:329
  41.7 1.3 %maximum_bitcast_fusion = f32[4096]{0:T(1024)} fusion(f32[32,128]{1,0:T(8,128)} %shard_map.28), kind=kLoop, calls=%fused_computation | loop fusion | flops 4096 | bytes 32768 | tf_op jit(solution)/shard_map/reshape | solution.py:365

commit v17 on v16

--- a/solution.py
+++ b/solution.py
@@ -131,6 +131,11 @@
             device_id_type=MESH,
         )
 
+    @pl.when(down)
+    def _():
+        remote(piece_ref, head, 2, (g - 1, 2)).start()
+        remote(piece_ref, head, 1, (g - 1, 0)).start()
+
     to_mate = remote(piece_ref, c, 0, (g, mate))
     to_mate.start()
 
@@ -138,11 +143,6 @@
         @pl.when(live)
         def _():
             remote(piece_ref, c, 3 + 3 * p, (g, p)).start()
-
-    @pl.when(down)
-    def _():
-        remote(piece_ref, head, 1, (g - 1, 0)).start()
-        remote(piece_ref, head, 2, (g - 1, 2)).start()
 
     @pl.when(g + 1 == n_rows)
     def _():

time: 43.3 us -> 43.2 us (level)
  no operation moved by 1% of the time
where the time goes in v17:
time: 43.2 us; the launch traced here: 42.9 us
  Pallas kernels  41.5 us (96%)
  other arithmetic  1.33 us (3%)
    pallas_call x1, Pallas kernels, fused_call(): pl.pallas_call(lambda *refs: fused_kernel(n_rows, n_cols, n_tiles, *refs)...  41.5 us
    reshape x1, other arithmetic, on_device(): return jnp.maximum(result, jnp.float32(-1.0)).reshape(piece)  1.33 us

profile of v17, /device:TPU:25, one launch (start us, length us, event | category | flops | bytes accessed | tf_op | source)
XLA Modules:
  0.0 42.9 jit_solution(4814349289976250823)
XLA Ops:
  0.0 41.5 %shard_map.28 = f32[32,128]{1,0:T(8,128)} custom-call(s32[3,64]{1,0:T(4,128)} %refs_0_.1, f32[32,128]{1,0:T(8,128)} %bitcast.3), custom_call_target="tpu_custom_call" | custom-call | flops 1610612736 | bytes 278528 | tf_op jit(solution)/shard_map/pallas_call | solution.py:329
  41.5 1.3 %maximum_bitcast_fusion = f32[4096]{0:T(1024)} fusion(f32[32,128]{1,0:T(8,128)} %shard_map.28), kind=kLoop, calls=%fused_computation | loop fusion | flops 4096 | bytes 32768 | tf_op jit(solution)/shard_map/reshape | solution.py:365

commit v18 on v17

--- a/solution.py
+++ b/solution.py
@@ -273,12 +273,15 @@
 
     base = c * SPILL
     acc = [jnp.full((8, 128), -1.0, jnp.float32) for _ in range(quads)]
-    for sender in range(n_cols):
-        @pl.when(sender != c)
-        def _():
-            all_results(sender, sender).wait_recv()
-
-        acc = gather_blocks([(sender, t) for t in range(n_tiles)], base, acc)
+    for side in (half, 1 - half):
+        for k in range(n_cols // 2):
+            sender = 4 * (k // 2) + 2 * side + (k % 2)
+
+            @pl.when(sender != c)
+            def _():
+                all_results(sender, sender).wait_recv()
+
+            acc = gather_blocks([(sender, t) for t in range(n_tiles)], base, acc)
 
     @pl.when(down)
     def _():

time: 43.2 us -> 43 us (level)
  no operation moved by 1% of the time
where the time goes in v18:
time: 43 us; the launch traced here: 42.7 us
  Pallas kernels  41.4 us (96%)
  other arithmetic  1.33 us (3%)
    pallas_call x1, Pallas kernels, fused_call(): pl.pallas_call(lambda *refs: fused_kernel(n_rows, n_cols, n_tiles, *refs)...  41.4 us
    reshape x1, other arithmetic, on_device(): return jnp.maximum(result, jnp.float32(-1.0)).reshape(piece)  1.33 us

profile of v18, /device:TPU:25, one launch (start us, length us, event | category | flops | bytes accessed | tf_op | source)
XLA Modules:
  0.0 42.7 jit_solution(392460593114882021)
XLA Ops:
  0.0 41.4 %shard_map.28 = f32[32,128]{1,0:T(8,128)} custom-call(s32[3,64]{1,0:T(4,128)} %refs_0_.1, f32[32,128]{1,0:T(8,128)} %bitcast.3), custom_call_target="tpu_custom_call" | custom-call | flops 1610612736 | bytes 278528 | tf_op jit(solution)/shard_map/pallas_call | solution.py:332
  41.4 1.3 %maximum_bitcast_fusion = f32[4096]{0:T(1024)} fusion(f32[32,128]{1,0:T(8,128)} %shard_map.28), kind=kLoop, calls=%fused_computation | loop fusion | flops 4096 | bytes 32768 | tf_op jit(solution)/shard_map/reshape | solution.py:368
